TPU v7x, 512 devices: a whole 4x8x8 slice. The times are simulated.
512 devices in a mesh: row: 64 (over z, y_lo, x), col: 8 (over y_hi, core).
Axes of the slice: x: 4, y: 8 (y_hi: 4, y_lo: 2; y = y_hi * 2 + y_lo), z: 8, core: 2. Of those that a mesh axis runs over, the one named last changes fastest.
Arguments:
- start_vectors: float32 [262144, 256], P('row', 'col'), may hold values from -6 to 6
- ham_blocks: float32 [2048, 8, 128, 128], P(('row', 'col')), may hold values from -0.1875 to 0.1875
- block_cols: int32 [2048, 8], P(('row', 'col')), may hold values from 0 to 2047, as said below
- block_counts: int32 [2048], P(('row', 'col')), may hold values from 1 to 8, as said below
- check_weights: float32 [256], replicated, may hold values from -0.375 to 0.375
Outputs:
- filtered: float32 [262144, 256], P('row', 'col')
- checksum: float32 [262144], P(('row', 'col'))
Inputs may be any that keep to these rules, and one draw needn't show every extreme that they name: `block_cols`: slot j of block row b names block column (b + d) mod 2048 for offsets d that are distinct within the row and lie from -4 to 3; slot 0 names the block row itself (d = 0). Only the first block_counts[b] slots of block row b are part of the operator. The block rows of one thirty-second of the devices (at least one device) hold 8 live slots each, all block rows of such a device alike; every other block row holds 1 to 3.
All inputs are finite; a program needn't handle non-finite values.
Results may differ from a plain program's by a relative error of at most 0.0003.
Values sent between devices are 32-bit elements; how exact they have to be, the bound alone decides.
No kernel may reach another device: no remote copies, remote signals or barrier semaphores. Data moves between devices by JAX's collectives and lax.ppermute only.
A program may use at most 64 MiB of HBM per device.

v0:
```python
import functools

import jax
import jax.numpy as jnp
from jax import lax
from jax.experimental import pallas as pl
from jax.experimental.pallas import tpu as pltpu
from jax.sharding import Mesh
from jax.sharding import PartitionSpec as P

REACH = 4
ITERS = 3
CENTRE = 0.25
HALF_WIDTH = 1.5
B = 128
CORES = 2
GROUP = 4
CHECK = 8

VMEM = pl.BlockSpec(memory_space=pltpu.VMEM)
SMEM = pl.BlockSpec(memory_space=pltpu.SMEM)


def split(value):
    high = value.astype(jnp.bfloat16)
    low = (value - high.astype(jnp.float32)).astype(jnp.bfloat16)
    return high, low


def prepare_kernel(total, place, ints_own, ints_other, own, other, rhs, near_list, far_list):
    rows, cap = own.shape[0], own.shape[1]
    core, base = place[0], place[1]
    chip_rows = CORES * rows
    rhs[chip_rows * cap] = jnp.zeros(rhs.shape[1:], rhs.dtype)
    near = jnp.int32(0)
    far = jnp.int32(0)
    for ints, blocks, side in ((ints_own, own, core), (ints_other, other, 1 - core)):
        for row in range(rows):
            chip_row = side * rows + row

            def one(slot, counts, ints=ints, blocks=blocks, row=row, chip_row=chip_row):
                near, far = counts
                high, low = split(blocks[row, slot].T)
                where = chip_row * cap + slot
                rhs[where, :, :B] = high
                rhs[where, :, B:] = low
                column = lax.rem(ints[row, slot] - base + total + total, total)
                is_left = column >= total - REACH
                is_near = column < chip_rows

                @pl.when(is_near)
                def _():
                    near_list[0, near] = chip_row
                    near_list[1, near] = where
                    near_list[2, near] = column

                @pl.when(jnp.logical_not(is_near))
                def _():
                    far_list[0, far] = chip_row
                    far_list[1, far] = where
                    far_list[2, far] = jnp.where(
                        is_left, column - (total - REACH), column - chip_rows + REACH
                    )

                step = is_near.astype(jnp.int32)
                return near + step, far + 1 - step

            near, far = lax.fori_loop(0, ints[row, cap], one, (near, far))
    for entries, used in ((near_list, near), (far_list, far)):
        for extra in range(GROUP - 1):
            entries[0, used + extra] = 0
            entries[1, used + extra] = chip_rows * cap
            entries[2, used + extra] = 0
        entries[3, 0] = lax.div(used + GROUP - 1, GROUP)


def stage(pieces, halves):
    width = halves.shape[1] - 16
    at = 0
    for piece, tiles in pieces:
        for tile in range(tiles):
            high, low = split(piece[tile * width : (tile + 1) * width, :])
            halves[at, :width, :B] = high
            halves[at, :width, B:] = low
            row = piece[tiles * width + tile : tiles * width + tile + 1, :]
            high, low = split(jnp.concatenate([row, jnp.zeros((15, B), jnp.float32)], 0))
            halves[at, width:, :B] = high
            halves[at, width:, B:] = low
            at += 1


def multiply(entries, rhs, halves, total):
    def group(index, carry):
        for member in range(GROUP):
            at = index * GROUP + member
            row = entries[0, at]
            matrix = rhs[entries[1, at]]
            result = jnp.dot(
                halves[entries[2, at]],
                jnp.concatenate([matrix, matrix], 0),
                preferred_element_type=jnp.float32,
            )
            total[row] = total[row] + (result[:, :B] + result[:, B:])
        return carry

    lax.fori_loop(0, entries[3, 0], group, 0)


def near_kernel(tiles, state, entries, rhs, total, halves):
    total[...] = jnp.zeros(total.shape, total.dtype)
    stage([(state, tiles)], halves)
    multiply(entries, rhs, halves, total)


def far_kernel(
    tiles, first, last, state, before, near_total, left, right, entries, rhs, *refs
):
    if last:
        out, out_check, halves, total = refs
    else:
        following, to_left, to_right, halves, total = refs
    width = halves.shape[1] - 16
    right_tiles = REACH - 1
    total[...] = near_total[...]
    stage([(left, REACH), (right, right_tiles)], halves)
    multiply(entries, rhs, halves, total)
    for tile in range(tiles):
        here = slice(tile * width, (tile + 1) * width)
        check = slice(tiles * width + tile, tiles * width + tile + 1)
        pair = []
        for product, at in ((total[tile, :width, :], here), (total[tile, width : width + 1, :], check)):
            value = (product - CENTRE * state[at, :]) * (1.0 / HALF_WIDTH)
            if not first:
                value = 2.0 * value - before[at, :]
            pair.append(value)
        main, row = pair
        if last:
            parts = out.shape[0]
            each = width // parts
            for part in range(parts):
                out[part, tile] = main[part * each : (part + 1) * each, :]
            out_check[tile : tile + 1, :] = row
        else:
            following[here, :] = main
            following[check, :] = row
            if tile < right_tiles:
                to_left[here, :] = main
                spot = right_tiles * width + tile
                to_left[spot : spot + 1, :] = row
            if tile >= tiles - REACH:
                shifted = tile - (tiles - REACH)
                to_right[shifted * width : (shifted + 1) * width, :] = main
                spot = REACH * width + shifted
                to_right[spot : spot + 1, :] = row


def gather_kernel(tiles, arrived, weights, state, to_left, to_right):
    parts, each = arrived.shape[0], arrived.shape[2]
    width = parts * each
    right_tiles = REACH - 1
    for tile in range(tiles):
        row = jnp.zeros((1, B), jnp.float32)
        for part in range(parts):
            value = arrived[part, tile]
            at = part * each
            row = row + jnp.sum(value * weights[at : at + each, :], axis=0, keepdims=True)
            state[tile * width + at : tile * width + at + each, :] = value
            if tile < right_tiles:
                to_left[tile * width + at : tile * width + at + each, :] = value
            if tile >= tiles - REACH:
                shifted = (tile - (tiles - REACH)) * width + at
                to_right[shifted : shifted + each, :] = value
        spot = tiles * width + tile
        state[spot : spot + 1, :] = row
        if tile < right_tiles:
            spot = right_tiles * width + tile
            to_left[spot : spot + 1, :] = row
        if tile >= tiles - REACH:
            spot = REACH * width + tile - (tiles - REACH)
            to_right[spot : spot + 1, :] = row


def call(kernel, shapes, inputs, scratch=(), flops=0, moved=0):
    return pl.pallas_call(
        kernel,
        out_shape=tuple(jax.ShapeDtypeStruct(shape, dtype) for shape, dtype, _ in shapes),
        in_specs=[spec for _, spec in inputs],
        out_specs=tuple(spec for _, _, spec in shapes),
        scratch_shapes=list(scratch),
        compiler_params=pltpu.CompilerParams(vmem_limit_bytes=40 << 20),
        cost_estimate=pl.CostEstimate(flops=flops, bytes_accessed=moved, transcendentals=0),
    )(*[value for value, _ in inputs])


def shift(value, axes, count, steps):
    return lax.ppermute(value, axes, [(at, (at + steps) % count) for at in range(count)])


def per_device(start_vectors, ham_blocks, block_cols, block_counts, check_weights):
    f32 = jnp.float32
    rows, cap = ham_blocks.shape[0], ham_blocks.shape[1]
    parts = lax.axis_size("part")
    chips = lax.axis_size(("row", "part"))
    core = lax.axis_index("core")
    chip = lax.axis_index(("row", "part"))
    tiles = CORES * rows
    total = chips * tiles
    each = start_vectors.shape[1]
    width = parts * each

    sent = start_vectors.T.reshape(each, parts, tiles, B).transpose(1, 2, 0, 3)
    arrived = lax.all_to_all(sent, "part", split_axis=0, concat_axis=0, tiled=True)
    ints = jnp.concatenate([block_cols, block_counts[:, None]], 1)
    other_ints = shift(ints, "core", CORES, 1)
    other_blocks = shift(ham_blocks, "core", CORES, 1)
    place = jnp.stack([core, chip * tiles]).astype(jnp.int32)
    length = tiles * cap + GROUP

    rhs, near_list, far_list = call(
        functools.partial(prepare_kernel, total),
        (
            ((tiles * cap + 1, B, 2 * B), jnp.bfloat16, VMEM),
            ((4, length), jnp.int32, SMEM),
            ((4, length), jnp.int32, SMEM),
        ),
        [(place, SMEM), (ints, SMEM), (other_ints, SMEM), (ham_blocks, VMEM), (other_blocks, VMEM)],
        flops=10**7,
        moved=8 << 20,
    )
    mine = lax.dynamic_index_in_dim(check_weights.reshape(parts, CORES, each), core, 1, False)
    weights = jnp.broadcast_to(mine.reshape(width, 1), (width, B))
    sizes = [tiles * width + CHECK, (REACH - 1) * width + CHECK, REACH * width + CHECK]
    pieces = tuple(((size, B), f32, VMEM) for size in sizes)
    state, to_left, to_right = call(
        functools.partial(gather_kernel, tiles), pieces, [(arrived, VMEM), (weights, VMEM)]
    )
    before = state
    for step in range(ITERS):
        first, last = step == 0, step == ITERS - 1
        left = shift(to_right, ("row", "part"), chips, 1)
        right = shift(to_left, ("row", "part"), chips, -1)
        (near_total,) = call(
            functools.partial(near_kernel, tiles),
            (((tiles, width + 16, B), f32, VMEM),),
            [(state, VMEM), (near_list, SMEM), (rhs, VMEM)],
            [pltpu.VMEM((tiles, width + 16, 2 * B), jnp.bfloat16)],
            flops=10**9,
            moved=4 << 20,
        )
        shapes = pieces
        if last:
            shapes = (
                ((parts, tiles, each, B), f32, VMEM),
                ((tiles, B), f32, VMEM),
            )
        results = call(
            functools.partial(far_kernel, tiles, first, last),
            shapes,
            [
                (state, VMEM),
                (before, VMEM),
                (near_total, VMEM),
                (left, VMEM),
                (right, VMEM),
                (far_list, SMEM),
                (rhs, VMEM),
            ],
            [
                pltpu.VMEM((2 * REACH - 1, width + 16, 2 * B), jnp.bfloat16),
                pltpu.VMEM((tiles, width + 16, B), f32),
            ],
            flops=10**9,
            moved=4 << 20,
        )
        if last:
            out, out_check = results
        else:
            before = state
            state, to_left, to_right = results
    returned = lax.all_to_all(out, "part", split_axis=0, concat_axis=0, tiled=True)
    checks = out_check + shift(out_check, "core", CORES, 1)
    checks = lax.dynamic_slice_in_dim(checks, core * rows, rows, 0).reshape(rows * B)
    filtered = returned.transpose(2, 0, 1, 3).reshape(each, parts * tiles * B).T
    return filtered, checks


def solution(mesh):
    names = ("row", "part", "core")
    rows, cols = mesh.devices.shape
    finer = Mesh(mesh.devices.reshape(rows, cols // CORES, CORES), names)
    placed = (
        P("row", ("part", "core")),
        P(names, None, None, None),
        P(names, None),
        P(names),
        P(),
    )
    return jax.shard_map(
        per_device,
        mesh=finer,
        in_specs=placed,
        out_specs=(P("row", ("part", "core")), P(names)),
        check_vma=False,
    )
```

profile of v0, /device:TPU:206, one launch (start us, length us, event | category | flops | bytes accessed | tf_op | source)
XLA Modules:
  0.0 117.7 jit_solution(5332371366945317282)
XLA Ops:
  0.6 0.0 copy-start
  0.6 0.0 copy-start.4
  0.7 0.0 copy-start.3
  0.7 0.0 copy-start.2
  0.7 2.1 %collective-permute-start.1 = (f32[4,8,128,128]{3,2,1,0:T(8,128)}, f32[4,8,128,128]{3,2,1,0:T(8,128)}, u32[]{:S(2)}, u32[]{:S(2)}) collective-permute-start(f32[4,8,128,128]{3,2,1,0:T(8,128)} %own.1), channel_id=1, source_target_pairs={{0,1},{1,0},{2,3},{3,2},{4,5},{5,4},{6,7},{7,6},{8,9},{9,8},{10,11... | collective-permute-start | bytes 6291464 | tf_op jit(solution)/shard_map/ppermute | solution.py:196
  2.7 1.1 copy.11
  3.9 1.1 copy.16
  5.0 6.2 %all-to-all-start = ((f32[4,8,32,128]{3,2,1,0:T(8,128)}), f32[4,8,32,128]{3,2,1,0:T(8,128)S(1)}, u32[]{:S(2)}, u32[]{:S(2)}) async-start(f32[4,8,32,128]{3,2,1,0:T(8,128)} %bitcast.20), calls=%async_computation | async-start | bytes 1048576 | tf_op jit(solution)/shard_map/all_to_all | solution.py:212
  11.2 0.0 copy-done.4
  11.2 0.1 copy.9
  11.3 0.1 reshape.20
  11.4 0.1 broadcast_in_dim.10
  11.5 15.7 %all-to-all-done.arrived = f32[4,8,32,128]{3,2,1,0:T(8,128)S(1)} async-done(((f32[4,8,32,128]{3,2,1,0:T(8,128)}), f32[4,8,32,128]{3,2,1,0:T(8,128)S(1)}, u32[]{:S(2)}, u32[]{:S(2)}) %all-to-all-start) | async-done | bytes 524320 | tf_op jit(solution)/shard_map/all_to_all | solution.py:212
  27.1 0.1 broadcast_in_dim.11.weights
  27.2 0.1 shard_map.68
  27.3 0.0 copy-start.1
  27.3 0.7 copy-done.1
  28.0 4.6 %collective-permute-start.2 = (f32[520,128]{1,0:T(8,128)S(1)}, f32[520,128]{1,0:T(8,128)S(1)}, u32[]{:S(2)}, u32[]{:S(2)}) collective-permute-start(f32[520,128]{1,0:T(8,128)S(1)} %get-tuple-element.19), channel_id=1, source_target_pairs={{0,2},{2,4},{4,6},{6,8},{8,10},{10,12},{12,14},{14,16},{16,18},{18... | collective-permute-start | bytes 798728 | tf_op jit(solution)/shard_map/ppermute | solution.py:196
  32.6 0.1 pad_add_fusion.ints_own
  32.6 1.9 %collective-permute-start = (s32[4,9]{1,0:T(4,128)S(1)}, s32[4,9]{1,0:T(4,128)S(1)}, u32[]{:S(2)}, u32[]{:S(2)}) collective-permute-start(s32[4,9]{1,0:T(4,128)S(1)} %pad_add_fusion.ints_own), channel_id=1, source_target_pairs={{0,1},{1,0},{2,3},{3,2},{4,5},{5,4},{6,7},{7,6},{8,9},{9,8},{10,11... | collective-permute-start | bytes 440 | tf_op jit(solution)/shard_map/ppermute | solution.py:196
  34.6 4.3 %collective-permute-start.3 = (f32[392,128]{1,0:T(8,128)}, f32[392,128]{1,0:T(8,128)S(1)}, u32[]{:S(2)}, u32[]{:S(2)}) collective-permute-start(f32[392,128]{1,0:T(8,128)} %copy-done.1), channel_id=1, source_target_pairs={{0,510},{2,0},{4,2},{6,4},{8,6},{10,8},{12,10},{14,12},{16,14},{18... | collective-permute-start | bytes 602120 | tf_op jit(solution)/shard_map/ppermute | solution.py:196
  38.9 0.1 pad_add_fusion.1.place
  38.9 0.0 collective-permute-done.ints_other
  38.9 0.0 collective-permute-done.1.other
  38.9 3.9 %shard_map.69 = (bf16[65,128,256]{2,1,0:T(8,128)(2,1)S(1)}, s32[4,68]{1,0:T(4,128)S(1)}, s32[4,68]{1,0:T(4,128)S(1)}) custom-call(s32[2]{0:T(128)S(1)} %pad_add_fusion.1.place, s32[4,9]{1,0:T(4,128)S(1)} %pad_add_fusion.ints_own, s32[4,9]{1,0:T(4,128)S(1)} %collective-permute-done.ints_other, f32[4,8,128,128]{3,2,1,0:T(8,128)S(1)} %copy-done, ...), custom_call_target="tpu_custom_call" | custom-call | flops 10000000 | bytes 8388608 | tf_op jit(solution)/shard_map/pallas_call | solution.py:184
  42.9 1.7 %shard_map.70.near_total = f32[8,144,128]{2,1,0:T(8,128)S(1)} custom-call(f32[1032,128]{1,0:T(8,128)S(1)} %get-tuple-element.16.state.before, s32[4,68]{1,0:T(4,128)S(1)} %get-tuple-element.17.entries, bf16[65,128,256]{2,1,0:T(8,128)(2,1)S(1)} %get-tuple-element.18.rhs), custom_call_target="tpu_custom_call" | custom-call | flops 1000000000 | bytes 4194304 | tf_op jit(solution)/shard_map/pallas_call | solution.py:184
  44.6 4.7 %collective-permute-done.3.right = f32[392,128]{1,0:T(8,128)S(1)} collective-permute-done((f32[392,128]{1,0:T(8,128)}, f32[392,128]{1,0:T(8,128)S(1)}, u32[]{:S(2)}, u32[]{:S(2)}) %collective-permute-start.3) | collective-permute-done | bytes 200736 | tf_op jit(solution)/shard_map/ppermute | solution.py:196
  49.3 0.0 collective-permute-done.2.left
  49.3 1.0 shard_map.71
  50.3 3.4 %collective-permute-start.4 = (f32[520,128]{1,0:T(8,128)S(1)}, f32[520,128]{1,0:T(8,128)S(1)}, u32[]{:S(2)}, u32[]{:S(2)}) collective-permute-start(f32[520,128]{1,0:T(8,128)S(1)} %get-tuple-element.23), channel_id=1, source_target_pairs={{0,2},{2,4},{4,6},{6,8},{8,10},{10,12},{12,14},{14,16},{16,18},{18... | collective-permute-start | bytes 798728 | tf_op jit(solution)/shard_map/ppermute | solution.py:196
  53.8 5.4 %collective-permute-start.5 = (f32[392,128]{1,0:T(8,128)S(1)}, f32[392,128]{1,0:T(8,128)S(1)}, u32[]{:S(2)}, u32[]{:S(2)}) collective-permute-start(f32[392,128]{1,0:T(8,128)S(1)} %get-tuple-element.24), channel_id=1, source_target_pairs={{0,510},{2,0},{4,2},{6,4},{8,6},{10,8},{12,10},{14,12},{16,14},{18... | collective-permute-start | bytes 602120 | tf_op jit(solution)/shard_map/ppermute | solution.py:196
  59.2 1.7 %shard_map.72.near_total = f32[8,144,128]{2,1,0:T(8,128)S(1)} custom-call(f32[1032,128]{1,0:T(8,128)S(1)} %get-tuple-element.22.state.before, s32[4,68]{1,0:T(4,128)S(1)} %get-tuple-element.17.entries, bf16[65,128,256]{2,1,0:T(8,128)(2,1)S(1)} %get-tuple-element.18.rhs), custom_call_target="tpu_custom_call" | custom-call | flops 1000000000 | bytes 4194304 | tf_op jit(solution)/shard_map/pallas_call | solution.py:184
  60.9 6.7 %collective-permute-done.5.right = f32[392,128]{1,0:T(8,128)S(1)} collective-permute-done((f32[392,128]{1,0:T(8,128)S(1)}, f32[392,128]{1,0:T(8,128)S(1)}, u32[]{:S(2)}, u32[]{:S(2)}) %collective-permute-start.5) | collective-permute-done | bytes 200736 | tf_op jit(solution)/shard_map/ppermute | solution.py:196
  67.6 1.3 %collective-permute-done.4.left = f32[520,128]{1,0:T(8,128)S(1)} collective-permute-done((f32[520,128]{1,0:T(8,128)S(1)}, f32[520,128]{1,0:T(8,128)S(1)}, u32[]{:S(2)}, u32[]{:S(2)}) %collective-permute-start.4) | collective-permute-done | bytes 266272 | tf_op jit(solution)/shard_map/ppermute | solution.py:196
  69.0 1.1 shard_map.73
  70.0 5.8 %collective-permute-start.6 = (f32[520,128]{1,0:T(8,128)S(1)}, f32[520,128]{1,0:T(8,128)S(1)}, u32[]{:S(2)}, u32[]{:S(2)}) collective-permute-start(f32[520,128]{1,0:T(8,128)S(1)} %get-tuple-element.26), channel_id=1, source_target_pairs={{0,2},{2,4},{4,6},{6,8},{8,10},{10,12},{12,14},{14,16},{16,18},{18... | collective-permute-start | bytes 798728 | tf_op jit(solution)/shard_map/ppermute | solution.py:196
  75.8 3.0 %collective-permute-start.7 = (f32[392,128]{1,0:T(8,128)S(1)}, f32[392,128]{1,0:T(8,128)S(1)}, u32[]{:S(2)}, u32[]{:S(2)}) collective-permute-start(f32[392,128]{1,0:T(8,128)S(1)} %get-tuple-element.27), channel_id=1, source_target_pairs={{0,510},{2,0},{4,2},{6,4},{8,6},{10,8},{12,10},{14,12},{16,14},{18... | collective-permute-start | bytes 602120 | tf_op jit(solution)/shard_map/ppermute | solution.py:196
  78.9 1.7 %shard_map.74.near_total = f32[8,144,128]{2,1,0:T(8,128)S(1)} custom-call(f32[1032,128]{1,0:T(8,128)S(1)} %get-tuple-element.25.state, s32[4,68]{1,0:T(4,128)S(1)} %get-tuple-element.17.entries, bf16[65,128,256]{2,1,0:T(8,128)(2,1)S(1)} %get-tuple-element.18.rhs), custom_call_target="tpu_custom_call" | custom-call | flops 1000000000 | bytes 4194304 | tf_op jit(solution)/shard_map/pallas_call | solution.py:184
  80.6 9.4 %collective-permute-done.7.right = f32[392,128]{1,0:T(8,128)S(1)} collective-permute-done((f32[392,128]{1,0:T(8,128)S(1)}, f32[392,128]{1,0:T(8,128)S(1)}, u32[]{:S(2)}, u32[]{:S(2)}) %collective-permute-start.7) | collective-permute-done | bytes 200736 | tf_op jit(solution)/shard_map/ppermute | solution.py:196
  90.0 0.0 collective-permute-done.6.left
  90.0 1.9 %shard_map.75 = (f32[4,8,32,128]{3,2,1,0:T(8,128)}, f32[8,128]{1,0:T(8,128)S(1)}) custom-call(f32[1032,128]{1,0:T(8,128)S(1)} %get-tuple-element.25.state, f32[1032,128]{1,0:T(8,128)S(1)} %get-tuple-element.22.state.before, f32[8,144,128]{2,1,0:T(8,128)S(1)} %shard_map.74.near_total, f32[520,128]{1,0:T(8,128)S(1)} %collective-permute-done.6.left, ...), custom_call_target="tpu_custom_call" | custom-call | flops 1000000000 | bytes 4194304 | tf_op jit(solution)/shard_map/pallas_call | solution.py:184
  91.8 11.7 %all-to-all-start.1 = ((f32[4,8,32,128]{3,2,1,0:T(8,128)}), f32[4,8,32,128]{3,2,1,0:T(8,128)S(1)}, u32[]{:S(2)}, u32[]{:S(2)}) async-start(f32[4,8,32,128]{3,2,1,0:T(8,128)} %get-tuple-element.28), calls=%async_computation.1 | async-start | bytes 1048576 | tf_op jit(solution)/shard_map/all_to_all | solution.py:280
  103.5 1.9 %collective-permute-start.8 = (f32[8,128]{1,0:T(8,128)S(1)}, f32[8,128]{1,0:T(8,128)S(1)}, u32[]{:S(2)}, u32[]{:S(2)}) collective-permute-start(f32[8,128]{1,0:T(8,128)S(1)} %get-tuple-element.29), channel_id=1, source_target_pairs={{0,1},{1,0},{2,3},{3,2},{4,5},{5,4},{6,7},{7,6},{8,9},{9,8},{10,11... | collective-permute-start | bytes 12296 | tf_op jit(solution)/shard_map/ppermute | solution.py:196
  105.4 1.1 collective-permute-done.8
  106.6 0.6 dynamic-slice_bitcast_fusion
  107.2 9.1 %all-to-all-done.1 = f32[4,8,32,128]{3,2,1,0:T(8,128)S(1)} async-done(((f32[4,8,32,128]{3,2,1,0:T(8,128)}), f32[4,8,32,128]{3,2,1,0:T(8,128)S(1)}, u32[]{:S(2)}, u32[]{:S(2)}) %all-to-all-start.1) | async-done | bytes 524320 | tf_op jit(solution)/shard_map/all_to_all | solution.py:280
  116.3 0.3 copy.10
  116.6 1.1 copy.15
  (5 shorter events, 0.0 us)
Async XLA Ops:
  0.6 38.3 %copy-start = (f32[4,8,128,128]{3,2,1,0:T(8,128)S(1)}, f32[4,8,128,128]{3,2,1,0:T(8,128)}, u32[]{:S(2)}) copy-start(f32[4,8,128,128]{3,2,1,0:T(8,128)} %own.1) | copy-start | bytes 6291460
  0.6 10.5 %copy-start.4 = (s32[4]{0:T(128)S(1)}, s32[4]{0:T(128)}, u32[]{:S(2)}) copy-start(s32[4]{0:T(128)} %param.8) | copy-start | bytes 52
  0.7 10.6 %copy-start.3 = (f32[256]{0:T(256)S(1)}, f32[256]{0:T(256)}, u32[]{:S(2)}) copy-start(f32[256]{0:T(256)} %param.9) | copy-start | bytes 3076
  0.7 31.9 %copy-start.2 = (s32[4,8]{1,0:T(4,128)S(1)}, s32[4,8]{1,0:T(4,128)}, u32[]{:S(2)}) copy-start(s32[4,8]{1,0:T(4,128)} %param.7) | copy-start | bytes 388
  0.7 38.3 %collective-permute-start.1 = (f32[4,8,128,128]{3,2,1,0:T(8,128)}, f32[4,8,128,128]{3,2,1,0:T(8,128)}, u32[]{:S(2)}, u32[]{:S(2)}) collective-permute-start(f32[4,8,128,128]{3,2,1,0:T(8,128)} %own.1), channel_id=1, source_target_pairs={{0,1},{1,0},{2,3},{3,2},{4,5},{5,4},{6,7},{7,6},{8,9},{9,8},{10,11... | collective-permute-start | bytes 6291464 | tf_op jit(solution)/shard_map/ppermute | solution.py:196
  5.0 22.1 %all-to-all-start = ((f32[4,8,32,128]{3,2,1,0:T(8,128)}), f32[4,8,32,128]{3,2,1,0:T(8,128)S(1)}, u32[]{:S(2)}, u32[]{:S(2)}) async-start(f32[4,8,32,128]{3,2,1,0:T(8,128)} %bitcast.20), calls=%async_computation | async-start | bytes 1048576 | tf_op jit(solution)/shard_map/all_to_all | solution.py:212
  27.3 0.7 copy-start.1
  28.0 21.3 %collective-permute-start.2 = (f32[520,128]{1,0:T(8,128)S(1)}, f32[520,128]{1,0:T(8,128)S(1)}, u32[]{:S(2)}, u32[]{:S(2)}) collective-permute-start(f32[520,128]{1,0:T(8,128)S(1)} %get-tuple-element.19), channel_id=1, source_target_pairs={{0,2},{2,4},{4,6},{6,8},{8,10},{10,12},{12,14},{14,16},{16,18},{18... | collective-permute-start | bytes 798728 | tf_op jit(solution)/shard_map/ppermute | solution.py:196
  32.6 6.3 %collective-permute-start = (s32[4,9]{1,0:T(4,128)S(1)}, s32[4,9]{1,0:T(4,128)S(1)}, u32[]{:S(2)}, u32[]{:S(2)}) collective-permute-start(s32[4,9]{1,0:T(4,128)S(1)} %pad_add_fusion.ints_own), channel_id=1, source_target_pairs={{0,1},{1,0},{2,3},{3,2},{4,5},{5,4},{6,7},{7,6},{8,9},{9,8},{10,11... | collective-permute-start | bytes 440 | tf_op jit(solution)/shard_map/ppermute | solution.py:196
  34.6 14.7 %collective-permute-start.3 = (f32[392,128]{1,0:T(8,128)}, f32[392,128]{1,0:T(8,128)S(1)}, u32[]{:S(2)}, u32[]{:S(2)}) collective-permute-start(f32[392,128]{1,0:T(8,128)} %copy-done.1), channel_id=1, source_target_pairs={{0,510},{2,0},{4,2},{6,4},{8,6},{10,8},{12,10},{14,12},{16,14},{18... | collective-permute-start | bytes 602120 | tf_op jit(solution)/shard_map/ppermute | solution.py:196
  50.3 18.6 %collective-permute-start.4 = (f32[520,128]{1,0:T(8,128)S(1)}, f32[520,128]{1,0:T(8,128)S(1)}, u32[]{:S(2)}, u32[]{:S(2)}) collective-permute-start(f32[520,128]{1,0:T(8,128)S(1)} %get-tuple-element.23), channel_id=1, source_target_pairs={{0,2},{2,4},{4,6},{6,8},{8,10},{10,12},{12,14},{14,16},{16,18},{18... | collective-permute-start | bytes 798728 | tf_op jit(solution)/shard_map/ppermute | solution.py:196
  53.8 13.8 %collective-permute-start.5 = (f32[392,128]{1,0:T(8,128)S(1)}, f32[392,128]{1,0:T(8,128)S(1)}, u32[]{:S(2)}, u32[]{:S(2)}) collective-permute-start(f32[392,128]{1,0:T(8,128)S(1)} %get-tuple-element.24), channel_id=1, source_target_pairs={{0,510},{2,0},{4,2},{6,4},{8,6},{10,8},{12,10},{14,12},{16,14},{18... | collective-permute-start | bytes 602120 | tf_op jit(solution)/shard_map/ppermute | solution.py:196
  70.0 20.0 %collective-permute-start.6 = (f32[520,128]{1,0:T(8,128)S(1)}, f32[520,128]{1,0:T(8,128)S(1)}, u32[]{:S(2)}, u32[]{:S(2)}) collective-permute-start(f32[520,128]{1,0:T(8,128)S(1)} %get-tuple-element.26), channel_id=1, source_target_pairs={{0,2},{2,4},{4,6},{6,8},{8,10},{10,12},{12,14},{14,16},{16,18},{18... | collective-permute-start | bytes 798728 | tf_op jit(solution)/shard_map/ppermute | solution.py:196
  75.8 14.1 %collective-permute-start.7 = (f32[392,128]{1,0:T(8,128)S(1)}, f32[392,128]{1,0:T(8,128)S(1)}, u32[]{:S(2)}, u32[]{:S(2)}) collective-permute-start(f32[392,128]{1,0:T(8,128)S(1)} %get-tuple-element.27), channel_id=1, source_target_pairs={{0,510},{2,0},{4,2},{6,4},{8,6},{10,8},{12,10},{14,12},{16,14},{18... | collective-permute-start | bytes 602120 | tf_op jit(solution)/shard_map/ppermute | solution.py:196
  91.8 24.4 %all-to-all-start.1 = ((f32[4,8,32,128]{3,2,1,0:T(8,128)}), f32[4,8,32,128]{3,2,1,0:T(8,128)S(1)}, u32[]{:S(2)}, u32[]{:S(2)}) async-start(f32[4,8,32,128]{3,2,1,0:T(8,128)} %get-tuple-element.28), calls=%async_computation.1 | async-start | bytes 1048576 | tf_op jit(solution)/shard_map/all_to_all | solution.py:280
  103.5 3.0 %collective-permute-start.8 = (f32[8,128]{1,0:T(8,128)S(1)}, f32[8,128]{1,0:T(8,128)S(1)}, u32[]{:S(2)}, u32[]{:S(2)}) collective-permute-start(f32[8,128]{1,0:T(8,128)S(1)} %get-tuple-element.29), channel_id=1, source_target_pairs={{0,1},{1,0},{2,3},{3,2},{4,5},{5,4},{6,7},{7,6},{8,9},{9,8},{10,11... | collective-permute-start | bytes 12296 | tf_op jit(solution)/shard_map/ppermute | solution.py:196
where the time goes:
time: 118 us
  starting transfers between devices  50.3 us (43%)
  waiting for transfers between devices  48 us (41%)
  Pallas kernels  13.1 us (11%)
  local copies, waits for them, and re-layouts  5.28 us (4%)
    ppermute x9, starting transfers between devices, shift(): lax.ppermute(value, axes, [(at, (at + steps) % count) for at in range(cou...  32.4 us
    ppermute x9, waiting for transfers between devices, shift(): lax.ppermute(value, axes, [(at, (at + steps) % count) for at in range(cou...  23.2 us
    all_to_all x1, waiting for transfers between devices, per_device(): lax.all_to_all(sent, 'part', split_axis=0, concat_axis=0, tiled=True)  15.7 us
    pallas_call x8, Pallas kernels, call(): pl.pallas_call(kernel, out_shape=tuple((jax.ShapeDtypeStruct(shape, dtype...  13.1 us
    all_to_all x1, starting transfers between devices, per_device(): lax.all_to_all(out, 'part', split_axis=0, concat_axis=0, tiled=True)  11.7 us
    all_to_all x1, waiting for transfers between devices, per_device(): lax.all_to_all(out, 'part', split_axis=0, concat_axis=0, tiled=True)  9.11 us
    all_to_all x1, starting transfers between devices, per_device(): lax.all_to_all(sent, 'part', split_axis=0, concat_axis=0, tiled=True)  6.19 us
    unnamed x12, local copies, waits for them, and re-layouts  2.93 us
  transfers between devices with their start and end apart: 11, of which 7 were waited for; matrix products, arithmetic and copies ran while one was open for 3% of the time, Pallas kernels for 8%

commit v1 on v0

v1 whole, which is shorter than its diff:
```python
import functools

import jax
import jax.numpy as jnp
from jax import lax
from jax.experimental import pallas as pl
from jax.experimental.pallas import tpu as pltpu
from jax.sharding import Mesh
from jax.sharding import PartitionSpec as P

REACH = 4
ITERS = 3
CENTRE = 0.25
HALF_WIDTH = 1.5
B = 128
CORES = 2
GROUP = 4
CHECK = 8

VMEM = pl.BlockSpec(memory_space=pltpu.VMEM)
SMEM = pl.BlockSpec(memory_space=pltpu.SMEM)


def split(value):
    high = value.astype(jnp.bfloat16)
    low = (value - high.astype(jnp.float32)).astype(jnp.bfloat16)
    return high, low


def prepare_kernel(total, place, ints_own, ints_other, own, other, rhs, near_list, low_list, high_list):
    rows, cap = own.shape[0], own.shape[1]
    core, base = place[0], place[1]
    chip_rows = CORES * rows
    rhs[chip_rows * cap] = jnp.zeros(rhs.shape[1:], rhs.dtype)
    lists = (near_list, low_list, high_list)
    used = (jnp.int32(0),) * 3
    for ints, blocks, side in ((ints_own, own, core), (ints_other, other, 1 - core)):
        for row in range(rows):
            chip_row = side * rows + row

            def one(slot, used, ints=ints, blocks=blocks, row=row, chip_row=chip_row):
                high, low = split(blocks[row, slot].T)
                where = chip_row * cap + slot
                rhs[where, :, :B] = high
                rhs[where, :, B:] = low
                column = lax.rem(ints[row, slot] - base + total + total, total)
                is_left = column >= total - REACH
                is_right = jnp.logical_and(column >= chip_rows, jnp.logical_not(is_left))
                is_near = column < chip_rows
                targets = (
                    (is_near, chip_row, column),
                    (is_left, chip_row, column - (total - REACH)),
                    (is_right, chip_row - (chip_rows - REACH), column - chip_rows),
                )
                following = []
                for entries, count, (chosen, line, tile) in zip(lists, used, targets):

                    @pl.when(chosen)
                    def _(entries=entries, count=count, line=line, tile=tile):
                        entries[0, count] = line
                        entries[1, count] = where
                        entries[2, count] = tile

                    following.append(count + chosen.astype(jnp.int32))
                return tuple(following)

            used = lax.fori_loop(0, ints[row, cap], one, used)
    for entries, count in zip(lists, used):
        for extra in range(GROUP - 1):
            entries[0, count + extra] = 0
            entries[1, count + extra] = chip_rows * cap
            entries[2, count + extra] = 0
        entries[3, 0] = lax.div(count + GROUP - 1, GROUP)


def stage(pieces, halves):
    width = halves.shape[1] - 16
    at = 0
    for piece in pieces:
        tiles = piece.shape[0] // width
        for tile in range(tiles):
            high, low = split(piece[tile * width : (tile + 1) * width, :])
            halves[at, :width, :B] = high
            halves[at, :width, B:] = low
            row = piece[tiles * width + tile : tiles * width + tile + 1, :]
            high, low = split(jnp.concatenate([row, jnp.zeros((15, B), jnp.float32)], 0))
            halves[at, width:, :B] = high
            halves[at, width:, B:] = low
            at += 1


def multiply(entries, rhs, halves, total):
    def group(index, carry):
        for member in range(GROUP):
            at = index * GROUP + member
            row = entries[0, at]
            matrix = rhs[entries[1, at]]
            result = jnp.dot(
                halves[entries[2, at]],
                jnp.concatenate([matrix, matrix], 0),
                preferred_element_type=jnp.float32,
            )
            total[row] = total[row] + (result[:, :B] + result[:, B:])
        return carry

    lax.fori_loop(0, entries[3, 0], group, 0)


def near_kernel(low, high, entries, rhs, low_total, high_total, halves, total):
    total[...] = jnp.zeros(total.shape, total.dtype)
    stage([low, high], halves)
    multiply(entries, rhs, halves, total)
    low_total[...] = total[:REACH]
    high_total[...] = total[REACH:]


def update(first, tile, state, before, total, width):
    here = slice(tile * width, (tile + 1) * width)
    check = slice(REACH * width + tile, REACH * width + tile + 1)
    pair = []
    for product, at in ((total[tile, :width, :], here), (total[tile, width : width + 1, :], check)):
        value = (product - CENTRE * state[at, :]) * (1.0 / HALF_WIDTH)
        if not first:
            value = 2.0 * value - before[at, :]
        pair.append(value)
    return pair


def far_kernel(first, state, before, near_total, halo, entries, rhs, *refs):
    halves, total = refs[-2:]
    width = halves.shape[1] - 16
    total[...] = near_total[...]
    stage([halo], halves)
    multiply(entries, rhs, halves, total)
    for tile in range(REACH):
        main, row = update(first, tile, state, before, total, width)
        for ref in refs[:-2]:
            tiles = ref.shape[0] // width
            if tile < tiles:
                ref[tile * width : (tile + 1) * width, :] = main
                ref[tiles * width + tile : tiles * width + tile + 1, :] = row


def last_kernel(place, state, before, near_total, halo, entries, rhs, high, *refs):
    halves, total, keep = refs[-3:]
    outs, checks = refs[:-4], refs[-4]
    parts = len(outs)
    width = halves.shape[1] - 16
    each = width // parts
    total[...] = near_total[...]
    stage([halo], halves)
    multiply(entries, rhs, halves, total)
    for tile in range(REACH):
        main, row = update(False, tile, state, before, total, width)
        keep[tile * width : (tile + 1) * width, :] = main
        checks[tile : tile + 1, :] = row
        spot = REACH * width + tile
        checks[REACH + tile : REACH + tile + 1, :] = high[spot : spot + 1, :]
    for steps, out in enumerate(outs):
        at = pl.multiple_of(lax.rem(place[2] + steps, parts) * each, each)
        for tile in range(REACH):
            out[tile] = keep[pl.ds(tile * width + at, each), :]
            out[REACH + tile] = high[pl.ds(tile * width + at, each), :]


def gather_kernel(place, weights, *refs):
    parts = weights.shape[0] // refs[0].shape[1]
    pieces, (low, low_message, high) = refs[:parts], refs[parts:]
    each = pieces[0].shape[1]
    width = parts * each
    for tile in range(2 * REACH):
        row = jnp.zeros((1, B), jnp.float32)
        ref, line = (low, tile) if tile < REACH else (high, tile - REACH)
        spot = REACH * width + line
        for steps, piece in enumerate(pieces):
            at = pl.multiple_of(lax.rem(place[2] - steps + parts, parts) * each, each)
            value = piece[tile]
            row = row + jnp.sum(value * weights[pl.ds(at, each), :], axis=0, keepdims=True)
            ref[pl.ds(line * width + at, each), :] = value
            if tile < REACH - 1:
                low_message[pl.ds(line * width + at, each), :] = value
        ref[spot : spot + 1, :] = row
        if tile < REACH - 1:
            spot = (REACH - 1) * width + tile
            low_message[spot : spot + 1, :] = row


def arrange_kernel(place, vectors, *refs):
    parts, tiles = len(refs), refs[0].shape[0]
    for steps, ref in enumerate(refs):
        at = lax.rem(place[2] + steps, parts) * (tiles * B)
        for tile in range(tiles):
            ref[tile] = vectors[:, pl.ds(pl.multiple_of(at + tile * B, B), B)]


def place_kernel(place, *refs):
    pieces, out = refs[:-1], refs[-1]
    parts, tiles = len(pieces), pieces[0].shape[0]
    for steps, piece in enumerate(pieces):
        at = lax.rem(place[2] - steps + parts, parts) * (tiles * B)
        for tile in range(tiles):
            out[:, pl.ds(pl.multiple_of(at + tile * B, B), B)] = piece[tile]


def call(kernel, shapes, inputs, scratch=(), flops=1, moved=1):
    return pl.pallas_call(
        kernel,
        out_shape=tuple(jax.ShapeDtypeStruct(shape, dtype) for shape, dtype, _ in shapes),
        in_specs=[spec for _, spec in inputs],
        out_specs=tuple(spec for _, _, spec in shapes),
        scratch_shapes=list(scratch),
        compiler_params=pltpu.CompilerParams(vmem_limit_bytes=16 << 20),
        cost_estimate=pl.CostEstimate(flops=flops, bytes_accessed=moved, transcendentals=0),
    )(*[value for value, _ in inputs])


def shift(value, axes, count, steps):
    return lax.ppermute(value, axes, [(at, (at + steps) % count) for at in range(count)])


def per_device(start_vectors, ham_blocks, block_cols, block_counts, check_weights):
    f32 = jnp.float32
    rows, cap = ham_blocks.shape[0], ham_blocks.shape[1]
    parts = lax.axis_size("part")
    chips = lax.axis_size(("row", "part"))
    core = lax.axis_index("core")
    chip = lax.axis_index(("row", "part"))
    tiles = CORES * rows
    total = chips * tiles
    each = start_vectors.shape[1]
    width = parts * each

    place = jnp.stack([core, chip * tiles, lax.axis_index("part")]).astype(jnp.int32)

    def exchange(pieces):
        moved = {steps: shift(pieces[steps], "part", parts, steps) for steps in (2, 1, 3)}
        return [pieces[0]] + [moved[steps] for steps in range(1, parts)]

    piece = ((tiles, each, B), f32, VMEM)
    sent = call(arrange_kernel, (piece,) * parts, [(place, SMEM), (start_vectors.T, VMEM)])
    arrived = exchange(sent)
    ints = jnp.concatenate([block_cols, block_counts[:, None]], 1)
    other_ints = shift(ints, "core", CORES, 1)
    other_blocks = shift(ham_blocks, "core", CORES, 1)
    list_shape = ((4, tiles * cap + GROUP), jnp.int32, SMEM)
    rhs, near_list, low_list, high_list = call(
        functools.partial(prepare_kernel, total),
        (((tiles * cap + 1, B, 2 * B), jnp.bfloat16, VMEM), list_shape, list_shape, list_shape),
        [(place, SMEM), (ints, SMEM), (other_ints, SMEM), (ham_blocks, VMEM), (other_blocks, VMEM)],
    )
    mine = lax.dynamic_index_in_dim(check_weights.reshape(parts, CORES, each), core, 1, False)
    weights = jnp.broadcast_to(mine.reshape(width, 1), (width, B))
    full = ((REACH * width + CHECK, B), f32, VMEM)
    fewer = (((REACH - 1) * width + CHECK, B), f32, VMEM)
    low, low_message, high = call(
        gather_kernel,
        (full, fewer, full),
        [(place, SMEM), (weights, VMEM)] + [(value, VMEM) for value in arrived],
    )
    low_before, high_before = low, high
    part_total = ((REACH, width + 16, B), f32, VMEM)
    for step in range(ITERS):
        first, last = step == 0, step == ITERS - 1
        left = shift(high, ("row", "part"), chips, 1)
        right = shift(low_message, ("row", "part"), chips, -1)
        low_total, high_total = call(
            near_kernel,
            (part_total, part_total),
            [(low, VMEM), (high, VMEM), (near_list, SMEM), (rhs, VMEM)],
            [
                pltpu.VMEM((tiles, width + 16, 2 * B), jnp.bfloat16),
                pltpu.VMEM((tiles, width + 16, B), f32),
            ],
        )

        scratch = [
            pltpu.VMEM((REACH, width + 16, 2 * B), jnp.bfloat16),
            pltpu.VMEM((REACH, width + 16, B), f32),
        ]

        def inputs(state, before, near_total, halo, entries):
            values = (state, before, near_total, halo)
            return [(value, VMEM) for value in values] + [(entries, SMEM), (rhs, VMEM)]

        kernel = functools.partial(far_kernel, first)
        (high_next,) = call(
            kernel, (full,), inputs(high, high_before, high_total, right, high_list), scratch
        )
        low_inputs = inputs(low, low_before, low_total, left, low_list)
        if last:
            *outs, checks = call(
                last_kernel,
                (piece,) * parts + (((tiles, B), f32, VMEM),),
                [(place, SMEM)] + low_inputs + [(high_next, VMEM)],
                scratch + [pltpu.VMEM((REACH * width, B), f32)],
            )
            break
        low_next, low_message = call(kernel, (full, fewer), low_inputs, scratch)
        low_before, high_before = low, high
        low, high = low_next, high_next
    returned = exchange(outs)
    (filtered,) = call(
        place_kernel,
        (((each, parts * tiles * B), f32, VMEM),),
        [(place, SMEM)] + [(value, VMEM) for value in returned],
    )
    checks = checks + shift(checks, "core", CORES, 1)
    checks = lax.dynamic_slice_in_dim(checks, core * rows, rows, 0).reshape(rows * B)
    return filtered.T, checks


def solution(mesh):
    names = ("row", "part", "core")
    rows, cols = mesh.devices.shape
    finer = Mesh(mesh.devices.reshape(rows, cols // CORES, CORES), names)
    placed = (
        P("row", ("part", "core")),
        P(names, None, None, None),
        P(names, None),
        P(names),
        P(),
    )
    return jax.shard_map(
        per_device,
        mesh=finer,
        in_specs=placed,
        out_specs=(P("row", ("part", "core")), P(names)),
        check_vma=False,
    )
```

time: 118 us -> 117 us (level)
  the two profiles are of different devices: /device:TPU:206 before, /device:TPU:1 now
where the time goes in v1:
time: 117 us
  starting transfers between devices  72.2 us (62%)
  waiting for transfers between devices  23.2 us (20%)
  Pallas kernels  14.8 us (13%)
  local copies, waits for them, and re-layouts  4.91 us (4%)
    ppermute x15, starting transfers between devices, shift(): lax.ppermute(value, axes, [(at, (at + steps) % count) for at in range(cou...  72.2 us
    ppermute x15, waiting for transfers between devices, shift(): lax.ppermute(value, axes, [(at, (at + steps) % count) for at in range(cou...  23.2 us
    pallas_call x13, Pallas kernels, call(): pl.pallas_call(kernel, out_shape=tuple((jax.ShapeDtypeStruct(shape, dtype...  14.8 us
    unnamed x4, local copies, waits for them, and re-layouts  2.63 us
  transfers between devices with their start and end apart: 15, of which 8 were waited for; matrix products, arithmetic and copies ran while one was open for 3% of the time, Pallas kernels for 11%

profile of v1, /device:TPU:1, one launch (start us, length us, event | category | flops | bytes accessed | tf_op | source)
XLA Modules:
  0.0 116.8 jit_solution(8062040195818209718)
XLA Ops:
  0.6 8.8 %collective-permute-start.4 = (f32[4,8,128,128]{3,2,1,0:T(8,128)}, f32[4,8,128,128]{3,2,1,0:T(8,128)S(1)}, u32[]{:S(2)}, u32[]{:S(2)}) collective-permute-start(f32[4,8,128,128]{3,2,1,0:T(8,128)} %own.1), channel_id=1, source_target_pairs={{0,1},{1,0},{2,3},{3,2},{4,5},{5,4},{6,7},{7,6},{8,9},{9,8},{10,11... | collective-permute-start | bytes 6291464 | tf_op jit(solution)/shard_map/ppermute | solution.py:218
  9.4 0.1 pad_add_fusion.1.place
  9.5 1.0 copy-done.1
  10.6 0.6 shard_map.68
  11.2 1.9 %collective-permute-start = (f32[8,32,128]{2,1,0:T(8,128)S(1)}, f32[8,32,128]{2,1,0:T(8,128)S(1)}, u32[]{:S(2)}, u32[]{:S(2)}) collective-permute-start(f32[8,32,128]{2,1,0:T(8,128)S(1)} %get-tuple-element.29), channel_id=1, source_target_pairs={{0,2},{2,4},{4,6},{6,0},{1,3},{3,5},{5,7},{7,1},{8,10},{10,12},{12... | collective-permute-start | bytes 393224 | tf_op jit(solution)/shard_map/ppermute | solution.py:218
  13.1 2.6 %collective-permute-start.1 = (f32[8,32,128]{2,1,0:T(8,128)S(1)}, f32[8,32,128]{2,1,0:T(8,128)S(1)}, u32[]{:S(2)}, u32[]{:S(2)}) collective-permute-start(f32[8,32,128]{2,1,0:T(8,128)S(1)} %get-tuple-element.30), channel_id=1, source_target_pairs={{0,4},{2,6},{4,0},{6,2},{1,5},{3,7},{5,1},{7,3},{8,12},{10,14},{12... | collective-permute-start | bytes 393224 | tf_op jit(solution)/shard_map/ppermute | solution.py:218
  15.7 5.0 %collective-permute-start.2 = (f32[8,32,128]{2,1,0:T(8,128)S(1)}, f32[8,32,128]{2,1,0:T(8,128)S(1)}, u32[]{:S(2)}, u32[]{:S(2)}) collective-permute-start(f32[8,32,128]{2,1,0:T(8,128)S(1)} %get-tuple-element.31), channel_id=1, source_target_pairs={{0,6},{2,0},{4,2},{6,4},{1,7},{3,1},{5,3},{7,5},{8,14},{10,8},{12,... | collective-permute-start | bytes 393224 | tf_op jit(solution)/shard_map/ppermute | solution.py:218
  20.7 0.8 reshape.13
  21.5 0.1 broadcast_in_dim.10
  21.5 0.9 collective-permute-done.refs_1_
  22.5 2.0 %collective-permute-done.1.refs_2_ = f32[8,32,128]{2,1,0:T(8,128)S(1)} collective-permute-done((f32[8,32,128]{2,1,0:T(8,128)S(1)}, f32[8,32,128]{2,1,0:T(8,128)S(1)}, u32[]{:S(2)}, u32[]{:S(2)}) %collective-permute-start.1) | collective-permute-done | bytes 131104 | tf_op jit(solution)/shard_map/ppermute | solution.py:218
  24.5 4.3 %collective-permute-done.2.refs_3_ = f32[8,32,128]{2,1,0:T(8,128)S(1)} collective-permute-done((f32[8,32,128]{2,1,0:T(8,128)S(1)}, f32[8,32,128]{2,1,0:T(8,128)S(1)}, u32[]{:S(2)}, u32[]{:S(2)}) %collective-permute-start.2) | collective-permute-done | bytes 131104 | tf_op jit(solution)/shard_map/ppermute | solution.py:218
  28.7 0.1 broadcast_in_dim.11.weights
  28.8 0.6 shard_map.69
  29.5 4.2 %collective-permute-start.5 = (f32[520,128]{1,0:T(8,128)S(1)}, f32[520,128]{1,0:T(8,128)S(1)}, u32[]{:S(2)}, u32[]{:S(2)}) collective-permute-start(f32[520,128]{1,0:T(8,128)S(1)} %get-tuple-element.33.high.state.before), channel_id=1, source_target_pairs={{0,2},{2,4},{4,6},{6,8},{8,10},{10,12},{12,14},{14,16},{16,18},{18... | collective-permute-start | bytes 798728 | tf_op jit(solution)/shard_map/ppermute | solution.py:218
  33.7 9.3 %collective-permute-start.6 = (f32[392,128]{1,0:T(8,128)S(1)}, f32[392,128]{1,0:T(8,128)S(1)}, u32[]{:S(2)}, u32[]{:S(2)}) collective-permute-start(f32[392,128]{1,0:T(8,128)S(1)} %get-tuple-element.40), channel_id=1, source_target_pairs={{0,510},{2,0},{4,2},{6,4},{8,6},{10,8},{12,10},{14,12},{16,14},{18... | collective-permute-start | bytes 602120 | tf_op jit(solution)/shard_map/ppermute | solution.py:218
  43.0 0.7 copy.8
  43.8 0.8 pad_add_fusion.ints_own
  44.5 3.1 %collective-permute-start.3 = (s32[4,9]{1,0:T(4,128)S(1)}, s32[4,9]{1,0:T(4,128)S(1)}, u32[]{:S(2)}, u32[]{:S(2)}) collective-permute-start(s32[4,9]{1,0:T(4,128)S(1)} %pad_add_fusion.ints_own), channel_id=1, source_target_pairs={{0,1},{1,0},{2,3},{3,2},{4,5},{5,4},{6,7},{7,6},{8,9},{9,8},{10,11... | collective-permute-start | bytes 440 | tf_op jit(solution)/shard_map/ppermute | solution.py:218
  47.6 0.8 collective-permute-done.3.ints_other
  48.4 1.6 %copy-done = f32[4,8,128,128]{3,2,1,0:T(8,128)S(1)} copy-done((f32[4,8,128,128]{3,2,1,0:T(8,128)S(1)}, f32[4,8,128,128]{3,2,1,0:T(8,128)}, u32[]{:S(2)}) %copy-start) | copy-done | bytes 2097176
  50.0 2.8 %shard_map.70 = (bf16[65,128,256]{2,1,0:T(8,128)(2,1)S(1)}, s32[4,68]{1,0:T(4,128)S(1)}, s32[4,68]{1,0:T(4,128)S(1)}, s32[4,68]{1,0:T(4,128)S(1)}) custom-call(s32[3]{0:T(128)S(1)} %pad_add_fusion.1.place, s32[4,9]{1,0:T(4,128)S(1)} %pad_add_fusion.ints_own, s32[4,9]{1,0:T(4,128)S(1)} %collective-permute-done.3.ints_other, f32[4,8,128,128]{3,2,1,0:T(8,128)S(1)} %copy-done, ...), custom_call_target="tpu_custom_call" | custom-call | flops 1 | bytes 1 | tf_op jit(solution)/shard_map/pallas_call | solution.py:206
  52.8 1.5 %shard_map.71 = (f32[4,144,128]{2,1,0:T(8,128)S(1)}, f32[4,144,128]{2,1,0:T(8,128)S(1)}) custom-call(f32[520,128]{1,0:T(8,128)S(1)} %get-tuple-element.32.low.state.before, f32[520,128]{1,0:T(8,128)S(1)} %get-tuple-element.33.high.state.before, s32[4,68]{1,0:T(4,128)S(1)} %get-tuple-element.34.entries, bf16[65,128,256]{2,1,0:T(8,128)(2,1)S(1)} %get-tuple-element.35.rhs), custom_call_target="tpu_custom_call" | custom-call | flops 1 | bytes 1 | tf_op jit(solution)/shard_map/pallas_call | solution.py:206
  54.3 0.0 collective-permute-done.6.halo
  54.3 0.9 shard_map.73.high.state.before
  55.2 1.9 %collective-permute-start.7 = (f32[520,128]{1,0:T(8,128)S(1)}, f32[520,128]{1,0:T(8,128)S(1)}, u32[]{:S(2)}, u32[]{:S(2)}) collective-permute-start(f32[520,128]{1,0:T(8,128)S(1)} %shard_map.73.high.state.before), channel_id=1, source_target_pairs={{0,2},{2,4},{4,6},{6,8},{8,10},{10,12},{12,14},{14,16},{16,18},{18... | collective-permute-start | bytes 798728 | tf_op jit(solution)/shard_map/ppermute | solution.py:218
  57.2 0.7 shard_map.72
  57.9 9.1 %collective-permute-start.8 = (f32[392,128]{1,0:T(8,128)S(1)}, f32[392,128]{1,0:T(8,128)S(1)}, u32[]{:S(2)}, u32[]{:S(2)}) collective-permute-start(f32[392,128]{1,0:T(8,128)S(1)} %get-tuple-element.45), channel_id=1, source_target_pairs={{0,510},{2,0},{4,2},{6,4},{8,6},{10,8},{12,10},{14,12},{16,14},{18... | collective-permute-start | bytes 602120 | tf_op jit(solution)/shard_map/ppermute | solution.py:218
  66.9 1.5 %shard_map.74 = (f32[4,144,128]{2,1,0:T(8,128)S(1)}, f32[4,144,128]{2,1,0:T(8,128)S(1)}) custom-call(f32[520,128]{1,0:T(8,128)S(1)} %get-tuple-element.38.low.state.before, f32[520,128]{1,0:T(8,128)S(1)} %shard_map.73.high.state.before, s32[4,68]{1,0:T(4,128)S(1)} %get-tuple-element.34.entries, bf16[65,128,256]{2,1,0:T(8,128)(2,1)S(1)} %get-tuple-element.35.rhs), custom_call_target="tpu_custom_call" | custom-call | flops 1 | bytes 1 | tf_op jit(solution)/shard_map/pallas_call | solution.py:206
  68.4 7.3 %collective-permute-done.8.halo = f32[392,128]{1,0:T(8,128)S(1)} collective-permute-done((f32[392,128]{1,0:T(8,128)S(1)}, f32[392,128]{1,0:T(8,128)S(1)}, u32[]{:S(2)}, u32[]{:S(2)}) %collective-permute-start.8) | collective-permute-done | bytes 200736 | tf_op jit(solution)/shard_map/ppermute | solution.py:218
  75.7 0.9 shard_map.76.high.state
  76.7 1.9 %collective-permute-start.9 = (f32[520,128]{1,0:T(8,128)S(1)}, f32[520,128]{1,0:T(8,128)S(1)}, u32[]{:S(2)}, u32[]{:S(2)}) collective-permute-start(f32[520,128]{1,0:T(8,128)S(1)} %shard_map.76.high.state), channel_id=1, source_target_pairs={{0,2},{2,4},{4,6},{6,8},{8,10},{10,12},{12,14},{14,16},{16,18},{18... | collective-permute-start | bytes 798728 | tf_op jit(solution)/shard_map/ppermute | solution.py:218
  78.6 0.0 collective-permute-done.7.halo
  78.6 0.7 shard_map.75
  79.3 9.5 %collective-permute-start.10 = (f32[392,128]{1,0:T(8,128)S(1)}, f32[392,128]{1,0:T(8,128)S(1)}, u32[]{:S(2)}, u32[]{:S(2)}) collective-permute-start(f32[392,128]{1,0:T(8,128)S(1)} %get-tuple-element.48), channel_id=1, source_target_pairs={{0,510},{2,0},{4,2},{6,4},{8,6},{10,8},{12,10},{14,12},{16,14},{18... | collective-permute-start | bytes 602120 | tf_op jit(solution)/shard_map/ppermute | solution.py:218
  88.9 1.5 %shard_map.77 = (f32[4,144,128]{2,1,0:T(8,128)S(1)}, f32[4,144,128]{2,1,0:T(8,128)S(1)}) custom-call(f32[520,128]{1,0:T(8,128)S(1)} %get-tuple-element.43.low.state, f32[520,128]{1,0:T(8,128)S(1)} %shard_map.76.high.state, s32[4,68]{1,0:T(4,128)S(1)} %get-tuple-element.34.entries, bf16[65,128,256]{2,1,0:T(8,128)(2,1)S(1)} %get-tuple-element.35.rhs), custom_call_target="tpu_custom_call" | custom-call | flops 1 | bytes 1 | tf_op jit(solution)/shard_map/pallas_call | solution.py:206
  90.4 4.6 %collective-permute-done.10.halo = f32[392,128]{1,0:T(8,128)S(1)} collective-permute-done((f32[392,128]{1,0:T(8,128)S(1)}, f32[392,128]{1,0:T(8,128)S(1)}, u32[]{:S(2)}, u32[]{:S(2)}) %collective-permute-start.10) | collective-permute-done | bytes 200736 | tf_op jit(solution)/shard_map/ppermute | solution.py:218
  95.0 0.9 shard_map.78.high
  95.9 0.0 collective-permute-done.9.halo
  95.9 0.7 shard_map.79
  96.7 1.9 %collective-permute-start.11 = (f32[8,32,128]{2,1,0:T(8,128)S(1)}, f32[8,32,128]{2,1,0:T(8,128)S(1)}, u32[]{:S(2)}, u32[]{:S(2)}) collective-permute-start(f32[8,32,128]{2,1,0:T(8,128)S(1)} %get-tuple-element.50), channel_id=1, source_target_pairs={{0,2},{2,4},{4,6},{6,0},{1,3},{3,5},{5,7},{7,1},{8,10},{10,12},{12... | collective-permute-start | bytes 393224 | tf_op jit(solution)/shard_map/ppermute | solution.py:218
  98.6 1.9 %collective-permute-start.12 = (f32[8,32,128]{2,1,0:T(8,128)S(1)}, f32[8,32,128]{2,1,0:T(8,128)S(1)}, u32[]{:S(2)}, u32[]{:S(2)}) collective-permute-start(f32[8,32,128]{2,1,0:T(8,128)S(1)} %get-tuple-element.51), channel_id=1, source_target_pairs={{0,4},{2,6},{4,0},{6,2},{1,5},{3,7},{5,1},{7,3},{8,12},{10,14},{12... | collective-permute-start | bytes 393224 | tf_op jit(solution)/shard_map/ppermute | solution.py:218
  100.5 5.5 %collective-permute-start.13 = (f32[8,32,128]{2,1,0:T(8,128)S(1)}, f32[8,32,128]{2,1,0:T(8,128)S(1)}, u32[]{:S(2)}, u32[]{:S(2)}) collective-permute-start(f32[8,32,128]{2,1,0:T(8,128)S(1)} %get-tuple-element.52), channel_id=1, source_target_pairs={{0,6},{2,0},{4,2},{6,4},{1,7},{3,1},{5,3},{7,5},{8,14},{10,8},{12,... | collective-permute-start | bytes 393224 | tf_op jit(solution)/shard_map/ppermute | solution.py:218
  106.0 5.6 %collective-permute-start.14 = (f32[8,128]{1,0:T(8,128)S(1)}, f32[8,128]{1,0:T(8,128)S(1)}, u32[]{:S(2)}, u32[]{:S(2)}) collective-permute-start(f32[8,128]{1,0:T(8,128)S(1)} %get-tuple-element.53), channel_id=1, source_target_pairs={{0,1},{1,0},{2,3},{3,2},{4,5},{5,4},{6,7},{7,6},{8,9},{9,8},{10,11... | collective-permute-start | bytes 12296 | tf_op jit(solution)/shard_map/ppermute | solution.py:218
  111.6 0.8 collective-permute-done.14
  112.4 0.6 dynamic-slice_bitcast_fusion
  113.0 2.5 %collective-permute-done.13.refs_3_ = f32[8,32,128]{2,1,0:T(8,128)S(1)} collective-permute-done((f32[8,32,128]{2,1,0:T(8,128)S(1)}, f32[8,32,128]{2,1,0:T(8,128)S(1)}, u32[]{:S(2)}, u32[]{:S(2)}) %collective-permute-start.13) | collective-permute-done | bytes 131104 | tf_op jit(solution)/shard_map/ppermute | solution.py:218
  115.4 1.4 %shard_map.80 = f32[32,4096]{1,0:T(8,128)} custom-call(s32[3]{0:T(128)S(1)} %pad_add_fusion.1.place, f32[8,32,128]{2,1,0:T(8,128)S(1)} %get-tuple-element.49.refs_0_, f32[8,32,128]{2,1,0:T(8,128)S(1)} %collective-permute-done.11.refs_1_, f32[8,32,128]{2,1,0:T(8,128)S(1)} %collective-permute-done.12.refs_2_, f32[8,32,128]{2,1,0:T(8,128)S(1)} %collective-permute-done.13.refs_3_), custom_call_target="tpu_custom_call" | custom-call | flops 1 | bytes 1 | tf_op jit(solution)/shard_map/pallas_call | solution.py:206
  (8 shorter events, 0.0 us)
Async XLA Ops:
  0.6 47.8 %collective-permute-start.4 = (f32[4,8,128,128]{3,2,1,0:T(8,128)}, f32[4,8,128,128]{3,2,1,0:T(8,128)S(1)}, u32[]{:S(2)}, u32[]{:S(2)}) collective-permute-start(f32[4,8,128,128]{3,2,1,0:T(8,128)} %own.1), channel_id=1, source_target_pairs={{0,1},{1,0},{2,3},{3,2},{4,5},{5,4},{6,7},{7,6},{8,9},{9,8},{10,11... | collective-permute-start | bytes 6291464 | tf_op jit(solution)/shard_map/ppermute | solution.py:218
  9.5 1.0 copy-start.1
  11.2 11.3 %collective-permute-start = (f32[8,32,128]{2,1,0:T(8,128)S(1)}, f32[8,32,128]{2,1,0:T(8,128)S(1)}, u32[]{:S(2)}, u32[]{:S(2)}) collective-permute-start(f32[8,32,128]{2,1,0:T(8,128)S(1)} %get-tuple-element.29), channel_id=1, source_target_pairs={{0,2},{2,4},{4,6},{6,0},{1,3},{3,5},{5,7},{7,1},{8,10},{10,12},{12... | collective-permute-start | bytes 393224 | tf_op jit(solution)/shard_map/ppermute | solution.py:218
  13.1 11.4 %collective-permute-start.1 = (f32[8,32,128]{2,1,0:T(8,128)S(1)}, f32[8,32,128]{2,1,0:T(8,128)S(1)}, u32[]{:S(2)}, u32[]{:S(2)}) collective-permute-start(f32[8,32,128]{2,1,0:T(8,128)S(1)} %get-tuple-element.30), channel_id=1, source_target_pairs={{0,4},{2,6},{4,0},{6,2},{1,5},{3,7},{5,1},{7,3},{8,12},{10,14},{12... | collective-permute-start | bytes 393224 | tf_op jit(solution)/shard_map/ppermute | solution.py:218
  15.7 13.0 %collective-permute-start.2 = (f32[8,32,128]{2,1,0:T(8,128)S(1)}, f32[8,32,128]{2,1,0:T(8,128)S(1)}, u32[]{:S(2)}, u32[]{:S(2)}) collective-permute-start(f32[8,32,128]{2,1,0:T(8,128)S(1)} %get-tuple-element.31), channel_id=1, source_target_pairs={{0,6},{2,0},{4,2},{6,4},{1,7},{3,1},{5,3},{7,5},{8,14},{10,8},{12,... | collective-permute-start | bytes 393224 | tf_op jit(solution)/shard_map/ppermute | solution.py:218
  29.5 27.7 %collective-permute-start.5 = (f32[520,128]{1,0:T(8,128)S(1)}, f32[520,128]{1,0:T(8,128)S(1)}, u32[]{:S(2)}, u32[]{:S(2)}) collective-permute-start(f32[520,128]{1,0:T(8,128)S(1)} %get-tuple-element.33.high.state.before), channel_id=1, source_target_pairs={{0,2},{2,4},{4,6},{6,8},{8,10},{10,12},{12,14},{14,16},{16,18},{18... | collective-permute-start | bytes 798728 | tf_op jit(solution)/shard_map/ppermute | solution.py:218
  33.7 20.6 %collective-permute-start.6 = (f32[392,128]{1,0:T(8,128)S(1)}, f32[392,128]{1,0:T(8,128)S(1)}, u32[]{:S(2)}, u32[]{:S(2)}) collective-permute-start(f32[392,128]{1,0:T(8,128)S(1)} %get-tuple-element.40), channel_id=1, source_target_pairs={{0,510},{2,0},{4,2},{6,4},{8,6},{10,8},{12,10},{14,12},{16,14},{18... | collective-permute-start | bytes 602120 | tf_op jit(solution)/shard_map/ppermute | solution.py:218
  44.5 3.9 %collective-permute-start.3 = (s32[4,9]{1,0:T(4,128)S(1)}, s32[4,9]{1,0:T(4,128)S(1)}, u32[]{:S(2)}, u32[]{:S(2)}) collective-permute-start(s32[4,9]{1,0:T(4,128)S(1)} %pad_add_fusion.ints_own), channel_id=1, source_target_pairs={{0,1},{1,0},{2,3},{3,2},{4,5},{5,4},{6,7},{7,6},{8,9},{9,8},{10,11... | collective-permute-start | bytes 440 | tf_op jit(solution)/shard_map/ppermute | solution.py:218
  48.4 1.6 %copy-start = (f32[4,8,128,128]{3,2,1,0:T(8,128)S(1)}, f32[4,8,128,128]{3,2,1,0:T(8,128)}, u32[]{:S(2)}) copy-start(f32[4,8,128,128]{3,2,1,0:T(8,128)} %own.1) | copy-start | bytes 6291460
  55.2 23.4 %collective-permute-start.7 = (f32[520,128]{1,0:T(8,128)S(1)}, f32[520,128]{1,0:T(8,128)S(1)}, u32[]{:S(2)}, u32[]{:S(2)}) collective-permute-start(f32[520,128]{1,0:T(8,128)S(1)} %shard_map.73.high.state.before), channel_id=1, source_target_pairs={{0,2},{2,4},{4,6},{6,8},{8,10},{10,12},{12,14},{14,16},{16,18},{18... | collective-permute-start | bytes 798728 | tf_op jit(solution)/shard_map/ppermute | solution.py:218
  57.9 17.9 %collective-permute-start.8 = (f32[392,128]{1,0:T(8,128)S(1)}, f32[392,128]{1,0:T(8,128)S(1)}, u32[]{:S(2)}, u32[]{:S(2)}) collective-permute-start(f32[392,128]{1,0:T(8,128)S(1)} %get-tuple-element.45), channel_id=1, source_target_pairs={{0,510},{2,0},{4,2},{6,4},{8,6},{10,8},{12,10},{14,12},{16,14},{18... | collective-permute-start | bytes 602120 | tf_op jit(solution)/shard_map/ppermute | solution.py:218
  76.7 19.2 %collective-permute-start.9 = (f32[520,128]{1,0:T(8,128)S(1)}, f32[520,128]{1,0:T(8,128)S(1)}, u32[]{:S(2)}, u32[]{:S(2)}) collective-permute-start(f32[520,128]{1,0:T(8,128)S(1)} %shard_map.76.high.state), channel_id=1, source_target_pairs={{0,2},{2,4},{4,6},{6,8},{8,10},{10,12},{12,14},{14,16},{16,18},{18... | collective-permute-start | bytes 798728 | tf_op jit(solution)/shard_map/ppermute | solution.py:218
  79.3 15.6 %collective-permute-start.10 = (f32[392,128]{1,0:T(8,128)S(1)}, f32[392,128]{1,0:T(8,128)S(1)}, u32[]{:S(2)}, u32[]{:S(2)}) collective-permute-start(f32[392,128]{1,0:T(8,128)S(1)} %get-tuple-element.48), channel_id=1, source_target_pairs={{0,510},{2,0},{4,2},{6,4},{8,6},{10,8},{12,10},{14,12},{16,14},{18... | collective-permute-start | bytes 602120 | tf_op jit(solution)/shard_map/ppermute | solution.py:218
  96.7 16.3 %collective-permute-start.11 = (f32[8,32,128]{2,1,0:T(8,128)S(1)}, f32[8,32,128]{2,1,0:T(8,128)S(1)}, u32[]{:S(2)}, u32[]{:S(2)}) collective-permute-start(f32[8,32,128]{2,1,0:T(8,128)S(1)} %get-tuple-element.50), channel_id=1, source_target_pairs={{0,2},{2,4},{4,6},{6,0},{1,3},{3,5},{5,7},{7,1},{8,10},{10,12},{12... | collective-permute-start | bytes 393224 | tf_op jit(solution)/shard_map/ppermute | solution.py:218
  98.6 14.4 %collective-permute-start.12 = (f32[8,32,128]{2,1,0:T(8,128)S(1)}, f32[8,32,128]{2,1,0:T(8,128)S(1)}, u32[]{:S(2)}, u32[]{:S(2)}) collective-permute-start(f32[8,32,128]{2,1,0:T(8,128)S(1)} %get-tuple-element.51), channel_id=1, source_target_pairs={{0,4},{2,6},{4,0},{6,2},{1,5},{3,7},{5,1},{7,3},{8,12},{10,14},{12... | collective-permute-start | bytes 393224 | tf_op jit(solution)/shard_map/ppermute | solution.py:218
  100.5 14.9 %collective-permute-start.13 = (f32[8,32,128]{2,1,0:T(8,128)S(1)}, f32[8,32,128]{2,1,0:T(8,128)S(1)}, u32[]{:S(2)}, u32[]{:S(2)}) collective-permute-start(f32[8,32,128]{2,1,0:T(8,128)S(1)} %get-tuple-element.52), channel_id=1, source_target_pairs={{0,6},{2,0},{4,2},{6,4},{1,7},{3,1},{5,3},{7,5},{8,14},{10,8},{12,... | collective-permute-start | bytes 393224 | tf_op jit(solution)/shard_map/ppermute | solution.py:218
  106.0 6.4 %collective-permute-start.14 = (f32[8,128]{1,0:T(8,128)S(1)}, f32[8,128]{1,0:T(8,128)S(1)}, u32[]{:S(2)}, u32[]{:S(2)}) collective-permute-start(f32[8,128]{1,0:T(8,128)S(1)} %get-tuple-element.53), channel_id=1, source_target_pairs={{0,1},{1,0},{2,3},{3,2},{4,5},{5,4},{6,7},{7,6},{8,9},{9,8},{10,11... | collective-permute-start | bytes 12296 | tf_op jit(solution)/shard_map/ppermute | solution.py:218

commit v2 on v1

v2 whole, which is shorter than its diff:
```python
import functools

import jax
import jax.numpy as jnp
from jax import lax
from jax.experimental import pallas as pl
from jax.experimental.pallas import tpu as pltpu
from jax.sharding import Mesh
from jax.sharding import PartitionSpec as P

REACH = 4
ITERS = 3
CENTRE = 0.25
HALF_WIDTH = 1.5
B = 128
CORES = 2
GROUP = 4
CHECK = 8

VMEM = pl.BlockSpec(memory_space=pltpu.VMEM)
SMEM = pl.BlockSpec(memory_space=pltpu.SMEM)


def split(value):
    high = value.astype(jnp.bfloat16)
    low = (value - high.astype(jnp.float32)).astype(jnp.bfloat16)
    return high, low


def prepare_kernel(total, place, ints_own, ints_other, own, other, rhs, near_list, even_list, odd_list):
    rows, cap = own.shape[0], own.shape[1]
    core, base, swap = place[0], place[1], place[3]
    chip_rows = CORES * rows
    rhs[chip_rows * cap] = jnp.zeros(rhs.shape[1:], rhs.dtype)
    lists = (near_list, even_list, odd_list)
    used = (jnp.int32(0),) * 3
    for ints, blocks, side in ((ints_own, own, core), (ints_other, other, 1 - core)):
        for row in range(rows):
            chip_row = side * rows + row

            def one(slot, used, ints=ints, blocks=blocks, row=row, chip_row=chip_row):
                high, low = split(blocks[row, slot].T)
                where = chip_row * cap + slot
                rhs[where, :, :B] = high
                rhs[where, :, B:] = low
                column = lax.rem(ints[row, slot] - base + total + total, total)
                is_left = column >= total - REACH
                is_near = column < chip_rows
                tile = jnp.where(is_left, column - (total - REACH), column - chip_rows)
                is_even = jnp.logical_and(jnp.logical_not(is_near), is_left == (swap == 0))
                is_odd = jnp.logical_and(jnp.logical_not(is_near), is_left != (swap == 0))
                line = lax.rem(chip_row, REACH)
                targets = (
                    (is_near, lax.rem(chip_row + swap, 2 * REACH), lax.rem(column + swap, 2 * REACH)),
                    (is_even, line, tile),
                    (is_odd, line, tile),
                )
                following = []
                for entries, count, (chosen, line, tile) in zip(lists, used, targets):

                    @pl.when(chosen)
                    def _(entries=entries, count=count, line=line, tile=tile):
                        entries[0, count] = line
                        entries[1, count] = where
                        entries[2, count] = tile

                    following.append(count + chosen.astype(jnp.int32))
                return tuple(following)

            used = lax.fori_loop(0, ints[row, cap], one, used)
    for entries, count in zip(lists, used):
        for extra in range(GROUP - 1):
            entries[0, count + extra] = 0
            entries[1, count + extra] = chip_rows * cap
            entries[2, count + extra] = 0
        entries[3, 0] = lax.div(count + GROUP - 1, GROUP)


def stage(pieces, halves):
    width = halves.shape[1] - 16
    at = 0
    for piece in pieces:
        tiles = piece.shape[0] // width
        for tile in range(tiles):
            high, low = split(piece[tile * width : (tile + 1) * width, :])
            halves[at, :width, :B] = high
            halves[at, :width, B:] = low
            row = piece[tiles * width + tile : tiles * width + tile + 1, :]
            high, low = split(jnp.concatenate([row, jnp.zeros((15, B), jnp.float32)], 0))
            halves[at, width:, :B] = high
            halves[at, width:, B:] = low
            at += 1


def multiply(entries, rhs, halves, total):
    def group(index, carry):
        for member in range(GROUP):
            at = index * GROUP + member
            row = entries[0, at]
            matrix = rhs[entries[1, at]]
            result = jnp.dot(
                halves[entries[2, at]],
                jnp.concatenate([matrix, matrix], 0),
                preferred_element_type=jnp.float32,
            )
            total[row] = total[row] + (result[:, :B] + result[:, B:])
        return carry

    lax.fori_loop(0, entries[3, 0], group, 0)


def near_kernel(even, odd, entries, rhs, even_total, odd_total, halves, total):
    total[...] = jnp.zeros(total.shape, total.dtype)
    stage([even, odd], halves)
    multiply(entries, rhs, halves, total)
    even_total[...] = total[:REACH]
    odd_total[...] = total[REACH:]


def update(first, tile, state, before, total, width):
    here = slice(tile * width, (tile + 1) * width)
    check = slice(REACH * width + tile, REACH * width + tile + 1)
    pair = []
    for product, at in ((total[tile, :width, :], here), (total[tile, width : width + 1, :], check)):
        value = (product - CENTRE * state[at, :]) * (1.0 / HALF_WIDTH)
        if not first:
            value = 2.0 * value - before[at, :]
        pair.append(value)
    return pair


def far_kernel(first, state, before, near_total, halo, entries, rhs, out, halves, total):
    width = halves.shape[1] - 16
    total[...] = near_total[...]
    stage([halo], halves)
    multiply(entries, rhs, halves, total)
    for tile in range(REACH):
        main, row = update(first, tile, state, before, total, width)
        out[tile * width : (tile + 1) * width, :] = main
        out[REACH * width + tile : REACH * width + tile + 1, :] = row


def last_kernel(place, state, before, near_total, halo, entries, rhs, odd, *refs):
    halves, total, keep = refs[-3:]
    outs, checks = refs[:-4], refs[-4]
    parts = len(outs)
    width = halves.shape[1] - 16
    each = width // parts
    total[...] = near_total[...]
    stage([halo], halves)
    multiply(entries, rhs, halves, total)
    even_at, odd_at = place[3], REACH - place[3]
    for tile in range(REACH):
        main, row = update(False, tile, state, before, total, width)
        keep[tile * width : (tile + 1) * width, :] = main
        checks[pl.ds(even_at + tile, 1), :] = row
        spot = REACH * width + tile
        checks[pl.ds(odd_at + tile, 1), :] = odd[spot : spot + 1, :]
    for steps, out in enumerate(outs):
        at = pl.multiple_of(lax.rem(place[2] + steps * place[4] + parts, parts) * each, each)
        for tile in range(REACH):
            out[even_at + tile] = keep[pl.ds(tile * width + at, each), :]
            out[odd_at + tile] = odd[pl.ds(tile * width + at, each), :]


def gather_kernel(place, weights, *refs):
    parts = weights.shape[0] // refs[0].shape[1]
    pieces, halves = refs[:parts], refs[parts:]
    each = pieces[0].shape[1]
    width = parts * each
    for half, start in zip(halves, (place[3], REACH - place[3])):
        for tile in range(REACH):
            row = jnp.zeros((1, B), jnp.float32)
            for steps, piece in enumerate(pieces):
                at = pl.multiple_of(lax.rem(place[2] - steps * place[4] + parts, parts) * each, each)
                value = piece[start + tile]
                row = row + jnp.sum(value * weights[pl.ds(at, each), :], axis=0, keepdims=True)
                half[pl.ds(tile * width + at, each), :] = value
            spot = REACH * width + tile
            half[spot : spot + 1, :] = row


def arrange_kernel(place, vectors, *pieces):
    parts, tiles = len(pieces), pieces[0].shape[0]
    for steps, ref in enumerate(pieces):
        at = lax.rem(place[2] + steps * place[4] + parts, parts) * (tiles * B)
        for tile in range(tiles):
            ref[tile] = vectors[:, pl.ds(pl.multiple_of(at + tile * B, B), B)]


def integers_kernel(cols, counts, ints):
    rows, cap = cols.shape
    lane = lax.broadcasted_iota(jnp.int32, (1, B), 1)
    for row in range(rows):
        value = jnp.where(lane == cap, counts[row], 0)
        for slot in range(cap):
            value = jnp.where(lane == slot, cols[row, slot], value)
        ints[row : row + 1, :] = value


def place_kernel(place, checks, other_checks, *refs):
    pieces, (out, out_check) = refs[:-2], refs[-2:]
    parts, tiles = len(pieces), pieces[0].shape[0]
    for steps, piece in enumerate(pieces):
        at = lax.rem(place[2] - steps * place[4] + parts, parts) * (tiles * B)
        for tile in range(tiles):
            out[:, pl.ds(pl.multiple_of(at + tile * B, B), B)] = piece[tile]
    rows = out_check.shape[0]
    for row in range(rows):
        line = pl.ds(place[0] * rows + row, 1)
        out_check[row : row + 1, :] = checks[line, :] + other_checks[line, :]


def call(kernel, shapes, inputs, scratch=(), flops=1, moved=1):
    return pl.pallas_call(
        kernel,
        out_shape=tuple(jax.ShapeDtypeStruct(shape, dtype) for shape, dtype, _ in shapes),
        in_specs=[spec for _, spec in inputs],
        out_specs=tuple(spec for _, _, spec in shapes),
        scratch_shapes=list(scratch),
        compiler_params=pltpu.CompilerParams(vmem_limit_bytes=16 << 20),
        cost_estimate=pl.CostEstimate(flops=flops, bytes_accessed=moved, transcendentals=0),
    )(*[value for value, _ in inputs])


def shift(value, axes, count, steps):
    return lax.ppermute(value, axes, [(at, (at + steps) % count) for at in range(count)])


def per_device(start_vectors, ham_blocks, block_cols, block_counts, check_weights):
    f32 = jnp.float32
    rows, cap = ham_blocks.shape[0], ham_blocks.shape[1]
    parts = lax.axis_size("part")
    chips = lax.axis_size(("row", "part"))
    core = lax.axis_index("core")
    chip = lax.axis_index(("row", "part"))
    tiles = CORES * rows
    total = chips * tiles
    each = start_vectors.shape[1]
    width = parts * each

    swap = REACH * (1 - core)
    place = jnp.stack([core, chip * tiles, lax.axis_index("part"), swap, 1 - 2 * core]).astype(jnp.int32)

    def pairs(count, steps):
        return [
            (at * CORES + side, (at + steps * (1 - 2 * side)) % count * CORES + side)
            for at in range(count)
            for side in range(CORES)
        ]

    def exchange(pieces):
        moved = [
            lax.ppermute(pieces[steps], ("part", "core"), pairs(parts, steps))
            for steps in range(1, parts)
        ]
        return [pieces[0]] + moved

    def round_chips(value, steps):
        return lax.ppermute(value, ("row", "part", "core"), pairs(chips, steps))

    piece = ((tiles, each, B), f32, VMEM)
    sent = call(arrange_kernel, (piece,) * parts, [(place, SMEM), (start_vectors.T, VMEM)])
    arrived = exchange(sent)
    blocks, columns, counts, _ = lax.optimization_barrier(
        (ham_blocks, block_cols, block_counts, sent[0])
    )
    (ints,) = call(
        integers_kernel, (((rows, B), jnp.int32, VMEM),), [(columns, SMEM), (counts, SMEM)]
    )
    other_ints = shift(ints, "core", CORES, 1)
    other_blocks = shift(blocks, "core", CORES, 1)
    list_shape = ((4, tiles * cap + GROUP), jnp.int32, SMEM)
    rhs, near_list, even_list, odd_list = call(
        functools.partial(prepare_kernel, total),
        (((tiles * cap + 1, B, 2 * B), jnp.bfloat16, VMEM), list_shape, list_shape, list_shape),
        [(place, SMEM), (ints, SMEM), (other_ints, SMEM), (ham_blocks, VMEM), (other_blocks, VMEM)],
    )
    mine = lax.dynamic_index_in_dim(check_weights.reshape(parts, CORES, each), core, 1, False)
    weights = jnp.broadcast_to(mine.reshape(width, 1), (width, B))
    full = ((REACH * width + CHECK, B), f32, VMEM)
    placed, _ = lax.optimization_barrier((place, near_list))
    even, odd = call(
        gather_kernel,
        (full, full),
        [(placed, SMEM), (weights, VMEM)] + [(value, VMEM) for value in arrived],
    )
    even_before, odd_before = even, odd
    part_total = ((REACH, width + 16, B), f32, VMEM)
    scratch = [
        pltpu.VMEM((REACH, width + 16, 2 * B), jnp.bfloat16),
        pltpu.VMEM((REACH, width + 16, B), f32),
    ]
    for step in range(ITERS):
        first, last = step == 0, step == ITERS - 1
        odd_halo = round_chips(even, 1)
        even_halo = round_chips(odd, -1)
        even_total, odd_total = call(
            near_kernel,
            (part_total, part_total),
            [(even, VMEM), (odd, VMEM), (near_list, SMEM), (rhs, VMEM)],
            [
                pltpu.VMEM((tiles, width + 16, 2 * B), jnp.bfloat16),
                pltpu.VMEM((tiles, width + 16, B), f32),
            ],
        )

        def inputs(state, before, near_total, halo, entries):
            values = (state, before, near_total, halo)
            return [(value, VMEM) for value in values] + [(entries, SMEM), (rhs, VMEM)]

        kernel = functools.partial(far_kernel, first)
        (odd_next,) = call(
            kernel, (full,), inputs(odd, odd_before, odd_total, odd_halo, odd_list), scratch
        )
        even_inputs = inputs(even, even_before, even_total, even_halo, even_list)
        if last:
            *outs, checks = call(
                last_kernel,
                (piece,) * parts + (((tiles, B), f32, VMEM),),
                [(place, SMEM)] + even_inputs + [(odd_next, VMEM)],
                scratch + [pltpu.VMEM((REACH * width, B), f32)],
            )
            break
        (even_next,) = call(kernel, (full,), even_inputs, scratch)
        even_before, odd_before = even, odd
        even, odd = even_next, odd_next
    returned = exchange(outs)
    filtered, check_sums = call(
        place_kernel,
        (((each, parts * tiles * B), f32, VMEM), ((rows, B), f32, VMEM)),
        [(place, SMEM), (checks, VMEM), (shift(checks, "core", CORES, 1), VMEM)]
        + [(value, VMEM) for value in returned],
    )
    return filtered.T, check_sums.reshape(rows * B)


def solution(mesh):
    names = ("row", "part", "core")
    rows, cols = mesh.devices.shape
    finer = Mesh(mesh.devices.reshape(rows, cols // CORES, CORES), names)
    placed = (
        P("row", ("part", "core")),
        P(names, None, None, None),
        P(names, None),
        P(names),
        P(),
    )
    return jax.shard_map(
        per_device,
        mesh=finer,
        in_specs=placed,
        out_specs=(P("row", ("part", "core")), P(names)),
        check_vma=False,
    )
```

time: 117 us -> 116 us (level)
  the two profiles are of different devices: /device:TPU:1 before, /device:TPU:448 now
where the time goes in v2:
time: 116 us
  starting transfers between devices  64.5 us (56%)
  waiting for transfers between devices  27.9 us (24%)
  Pallas kernels  17.4 us (15%)
  local copies, waits for them, and re-layouts  5 us (4%)
    ppermute x6, starting transfers between devices, exchange(): lax.ppermute(pieces[steps], ('part', 'core'), pairs(parts, steps))  31.9 us
    ppermute x6, starting transfers between devices, round_chips(): return lax.ppermute(value, ('row', 'part', 'core'), pairs(chips, steps))  26.9 us
    ppermute x6, waiting for transfers between devices, round_chips(): return lax.ppermute(value, ('row', 'part', 'core'), pairs(chips, steps))  23.8 us
    pallas_call x14, Pallas kernels, call(): pl.pallas_call(kernel, out_shape=tuple((jax.ShapeDtypeStruct(shape, dtype...  17.4 us
    ppermute x3, starting transfers between devices, shift(): lax.ppermute(value, axes, [(at, (at + steps) % count) for at in range(cou...  5.76 us
    unnamed x8, local copies, waits for them, and re-layouts  3.97 us
    ppermute x6, waiting for transfers between devices, exchange(): lax.ppermute(pieces[steps], ('part', 'core'), pairs(parts, steps))  2.78 us
  transfers between devices with their start and end apart: 15, of which 7 were waited for; matrix products, arithmetic and copies ran while one was open for 1% of the time, Pallas kernels for 12%

profile of v2, /device:TPU:448, one launch (start us, length us, event | category | flops | bytes accessed | tf_op | source)
XLA Modules:
  0.0 115.7 jit_solution(18436280019450855085)
XLA Ops:
  0.6 0.1 stack.23.place
  0.7 1.0 copy-done.1
  1.8 0.6 shard_map.68
  2.4 1.9 %collective-permute-start.1 = (f32[4,8,128,128]{3,2,1,0:T(8,128)}, f32[4,8,128,128]{3,2,1,0:T(8,128)S(1)}, u32[]{:S(2)}, u32[]{:S(2)}) collective-permute-start(f32[4,8,128,128]{3,2,1,0:T(8,128)} %own.1), channel_id=1, source_target_pairs={{0,1},{1,0},{2,3},{3,2},{4,5},{5,4},{6,7},{7,6},{8,9},{9,8},{10,11... | collective-permute-start | bytes 6291464 | tf_op jit(solution)/shard_map/ppermute | solution.py:227
  4.3 4.5 %collective-permute-start.2 = (f32[8,32,128]{2,1,0:T(8,128)S(1)}, f32[8,32,128]{2,1,0:T(8,128)S(1)}, u32[]{:S(2)}, u32[]{:S(2)}) collective-permute-start(f32[8,32,128]{2,1,0:T(8,128)S(1)} %get-tuple-element.35), channel_id=1, source_target_pairs={{0,2},{1,7},{2,4},{3,1},{4,6},{5,3},{6,0},{7,5},{8,10},{9,15},{10,... | collective-permute-start | bytes 393224 | tf_op jit(solution)/shard_map/ppermute | solution.py:254
  8.8 5.9 %collective-permute-start.3 = (f32[8,32,128]{2,1,0:T(8,128)S(1)}, f32[8,32,128]{2,1,0:T(8,128)S(1)}, u32[]{:S(2)}, u32[]{:S(2)}) collective-permute-start(f32[8,32,128]{2,1,0:T(8,128)S(1)} %get-tuple-element.36), channel_id=1, source_target_pairs={{0,4},{1,5},{2,6},{3,7},{4,0},{5,1},{6,2},{7,3},{8,12},{9,13},{10,... | collective-permute-start | bytes 393224 | tf_op jit(solution)/shard_map/ppermute | solution.py:254
  14.8 5.3 %collective-permute-start.4 = (f32[8,32,128]{2,1,0:T(8,128)S(1)}, f32[8,32,128]{2,1,0:T(8,128)S(1)}, u32[]{:S(2)}, u32[]{:S(2)}) collective-permute-start(f32[8,32,128]{2,1,0:T(8,128)S(1)} %get-tuple-element.37), channel_id=1, source_target_pairs={{0,6},{1,3},{2,0},{3,5},{4,2},{5,7},{6,4},{7,1},{8,14},{9,11},{10,... | collective-permute-start | bytes 393224 | tf_op jit(solution)/shard_map/ppermute | solution.py:254
  20.0 0.0 copy-start.2
  20.0 0.7 copy-done.2
  20.7 0.7 copy-done.3
  21.4 0.6 shard_map.69.ints_own
  22.0 1.9 %collective-permute-start = (s32[4,128]{1,0:T(4,128)S(1)}, s32[4,128]{1,0:T(4,128)S(1)}, u32[]{:S(2)}, u32[]{:S(2)}) collective-permute-start(s32[4,128]{1,0:T(4,128)S(1)} %shard_map.69.ints_own), channel_id=1, source_target_pairs={{0,1},{1,0},{2,3},{3,2},{4,5},{5,4},{6,7},{7,6},{8,9},{9,8},{10,11... | collective-permute-start | bytes 6152 | tf_op jit(solution)/shard_map/ppermute | solution.py:227
  23.9 0.8 reshape.13
  24.7 0.1 broadcast_in_dim.7
  24.8 0.2 collective-permute-done.ints_other
  25.0 0.0 collective-permute-done.1.other
  25.0 1.6 %copy-done = f32[4,8,128,128]{3,2,1,0:T(8,128)S(1)} copy-done((f32[4,8,128,128]{3,2,1,0:T(8,128)S(1)}, f32[4,8,128,128]{3,2,1,0:T(8,128)}, u32[]{:S(2)}) %copy-start) | copy-done | bytes 2097176
  26.6 3.2 %shard_map.70 = (bf16[65,128,256]{2,1,0:T(8,128)(2,1)S(1)}, s32[4,68]{1,0:T(4,128)S(1)}, s32[4,68]{1,0:T(4,128)S(1)}, s32[4,68]{1,0:T(4,128)S(1)}) custom-call(s32[5]{0:T(128)S(1)} %stack.23.place, s32[4,128]{1,0:T(4,128)S(1)} %shard_map.69.ints_own, s32[4,128]{1,0:T(4,128)S(1)} %collective-permute-done.ints_other, f32[4,8,128,128]{3,2,1,0:T(8,128)S(1)} %copy-done, ...), custom_call_target="tpu_custom_call" | custom-call | flops 1 | bytes 1 | tf_op jit(solution)/shard_map/pallas_call | solution.py:215
  29.8 0.0 collective-permute-done.2.refs_1_
  29.8 0.0 collective-permute-done.3.refs_2_
  29.8 0.1 broadcast_in_dim.8.weights
  29.9 0.7 shard_map.71
  30.6 1.9 %collective-permute-start.6 = (f32[520,128]{1,0:T(8,128)S(1)}, f32[520,128]{1,0:T(8,128)S(1)}, u32[]{:S(2)}, u32[]{:S(2)}) collective-permute-start(f32[520,128]{1,0:T(8,128)S(1)} %get-tuple-element.38.even.state.before), channel_id=1, source_target_pairs={{0,2},{1,511},{2,4},{3,1},{4,6},{5,3},{6,8},{7,5},{8,10},{9,7},{10... | collective-permute-start | bytes 798728 | tf_op jit(solution)/shard_map/ppermute | solution.py:260
  32.5 8.1 %collective-permute-start.5 = (f32[520,128]{1,0:T(8,128)S(1)}, f32[520,128]{1,0:T(8,128)S(1)}, u32[]{:S(2)}, u32[]{:S(2)}) collective-permute-start(f32[520,128]{1,0:T(8,128)S(1)} %get-tuple-element.39.odd.state.before), channel_id=1, source_target_pairs={{0,510},{1,3},{2,0},{3,5},{4,2},{5,7},{6,4},{7,9},{8,6},{9,11},{10... | collective-permute-start | bytes 798728 | tf_op jit(solution)/shard_map/ppermute | solution.py:260
  40.6 1.7 %shard_map.72 = (f32[4,144,128]{2,1,0:T(8,128)S(1)}, f32[4,144,128]{2,1,0:T(8,128)S(1)}) custom-call(f32[520,128]{1,0:T(8,128)S(1)} %get-tuple-element.38.even.state.before, f32[520,128]{1,0:T(8,128)S(1)} %get-tuple-element.39.odd.state.before, s32[4,68]{1,0:T(4,128)S(1)} %get-tuple-element.33.entries, bf16[65,128,256]{2,1,0:T(8,128)(2,1)S(1)} %get-tuple-element.40.rhs), custom_call_target="tpu_custom_call" | custom-call | flops 1 | bytes 1 | tf_op jit(solution)/shard_map/pallas_call | solution.py:215
  42.4 8.7 %collective-permute-done.6.halo = f32[520,128]{1,0:T(8,128)S(1)} collective-permute-done((f32[520,128]{1,0:T(8,128)S(1)}, f32[520,128]{1,0:T(8,128)S(1)}, u32[]{:S(2)}, u32[]{:S(2)}) %collective-permute-start.6) | collective-permute-done | bytes 266272 | tf_op jit(solution)/shard_map/ppermute | solution.py:260
  51.1 0.9 shard_map.74.odd.state.before
  52.0 1.9 %collective-permute-start.7 = (f32[520,128]{1,0:T(8,128)S(1)}, f32[520,128]{1,0:T(8,128)S(1)}, u32[]{:S(2)}, u32[]{:S(2)}) collective-permute-start(f32[520,128]{1,0:T(8,128)S(1)} %shard_map.74.odd.state.before), channel_id=1, source_target_pairs={{0,510},{1,3},{2,0},{3,5},{4,2},{5,7},{6,4},{7,9},{8,6},{9,11},{10... | collective-permute-start | bytes 798728 | tf_op jit(solution)/shard_map/ppermute | solution.py:260
  53.9 0.9 shard_map.73.even.state.before
  54.9 4.8 %collective-permute-start.8 = (f32[520,128]{1,0:T(8,128)S(1)}, f32[520,128]{1,0:T(8,128)S(1)}, u32[]{:S(2)}, u32[]{:S(2)}) collective-permute-start(f32[520,128]{1,0:T(8,128)S(1)} %shard_map.73.even.state.before), channel_id=1, source_target_pairs={{0,2},{1,511},{2,4},{3,1},{4,6},{5,3},{6,8},{7,5},{8,10},{9,7},{10... | collective-permute-start | bytes 798728 | tf_op jit(solution)/shard_map/ppermute | solution.py:260
  59.7 1.7 %shard_map.75 = (f32[4,144,128]{2,1,0:T(8,128)S(1)}, f32[4,144,128]{2,1,0:T(8,128)S(1)}) custom-call(f32[520,128]{1,0:T(8,128)S(1)} %shard_map.73.even.state.before, f32[520,128]{1,0:T(8,128)S(1)} %shard_map.74.odd.state.before, s32[4,68]{1,0:T(4,128)S(1)} %get-tuple-element.33.entries, bf16[65,128,256]{2,1,0:T(8,128)(2,1)S(1)} %get-tuple-element.40.rhs), custom_call_target="tpu_custom_call" | custom-call | flops 1 | bytes 1 | tf_op jit(solution)/shard_map/pallas_call | solution.py:215
  61.5 8.3 %collective-permute-done.7.halo = f32[520,128]{1,0:T(8,128)S(1)} collective-permute-done((f32[520,128]{1,0:T(8,128)S(1)}, f32[520,128]{1,0:T(8,128)S(1)}, u32[]{:S(2)}, u32[]{:S(2)}) %collective-permute-start.7) | collective-permute-done | bytes 266272 | tf_op jit(solution)/shard_map/ppermute | solution.py:260
  69.8 1.0 shard_map.76.even.state
  70.8 1.9 %collective-permute-start.10 = (f32[520,128]{1,0:T(8,128)S(1)}, f32[520,128]{1,0:T(8,128)S(1)}, u32[]{:S(2)}, u32[]{:S(2)}) collective-permute-start(f32[520,128]{1,0:T(8,128)S(1)} %shard_map.76.even.state), channel_id=1, source_target_pairs={{0,2},{1,511},{2,4},{3,1},{4,6},{5,3},{6,8},{7,5},{8,10},{9,7},{10... | collective-permute-start | bytes 798728 | tf_op jit(solution)/shard_map/ppermute | solution.py:260
  72.7 1.0 shard_map.77.odd.state
  73.7 8.1 %collective-permute-start.9 = (f32[520,128]{1,0:T(8,128)S(1)}, f32[520,128]{1,0:T(8,128)S(1)}, u32[]{:S(2)}, u32[]{:S(2)}) collective-permute-start(f32[520,128]{1,0:T(8,128)S(1)} %shard_map.77.odd.state), channel_id=1, source_target_pairs={{0,510},{1,3},{2,0},{3,5},{4,2},{5,7},{6,4},{7,9},{8,6},{9,11},{10... | collective-permute-start | bytes 798728 | tf_op jit(solution)/shard_map/ppermute | solution.py:260
  81.8 1.7 %shard_map.78 = (f32[4,144,128]{2,1,0:T(8,128)S(1)}, f32[4,144,128]{2,1,0:T(8,128)S(1)}) custom-call(f32[520,128]{1,0:T(8,128)S(1)} %shard_map.76.even.state, f32[520,128]{1,0:T(8,128)S(1)} %shard_map.77.odd.state, s32[4,68]{1,0:T(4,128)S(1)} %get-tuple-element.33.entries, bf16[65,128,256]{2,1,0:T(8,128)(2,1)S(1)} %get-tuple-element.40.rhs), custom_call_target="tpu_custom_call" | custom-call | flops 1 | bytes 1 | tf_op jit(solution)/shard_map/pallas_call | solution.py:215
  83.6 1.5 %collective-permute-done.10.halo = f32[520,128]{1,0:T(8,128)S(1)} collective-permute-done((f32[520,128]{1,0:T(8,128)S(1)}, f32[520,128]{1,0:T(8,128)S(1)}, u32[]{:S(2)}, u32[]{:S(2)}) %collective-permute-start.10) | collective-permute-done | bytes 266272 | tf_op jit(solution)/shard_map/ppermute | solution.py:260
  85.1 1.0 shard_map.79.odd
  86.1 5.2 %collective-permute-done.9.halo = f32[520,128]{1,0:T(8,128)S(1)} collective-permute-done((f32[520,128]{1,0:T(8,128)S(1)}, f32[520,128]{1,0:T(8,128)S(1)}, u32[]{:S(2)}, u32[]{:S(2)}) %collective-permute-start.9) | collective-permute-done | bytes 266272 | tf_op jit(solution)/shard_map/ppermute | solution.py:260
  91.3 1.0 shard_map.80
  92.3 1.9 %collective-permute-start.12 = (f32[8,32,128]{2,1,0:T(8,128)S(1)}, f32[8,32,128]{2,1,0:T(8,128)S(1)}, u32[]{:S(2)}, u32[]{:S(2)}) collective-permute-start(f32[8,32,128]{2,1,0:T(8,128)S(1)} %get-tuple-element.51), channel_id=1, source_target_pairs={{0,2},{1,7},{2,4},{3,1},{4,6},{5,3},{6,0},{7,5},{8,10},{9,15},{10,... | collective-permute-start | bytes 393224 | tf_op jit(solution)/shard_map/ppermute | solution.py:254
  94.2 12.4 %collective-permute-start.13 = (f32[8,32,128]{2,1,0:T(8,128)S(1)}, f32[8,32,128]{2,1,0:T(8,128)S(1)}, u32[]{:S(2)}, u32[]{:S(2)}) collective-permute-start(f32[8,32,128]{2,1,0:T(8,128)S(1)} %get-tuple-element.52), channel_id=1, source_target_pairs={{0,4},{1,5},{2,6},{3,7},{4,0},{5,1},{6,2},{7,3},{8,12},{9,13},{10,... | collective-permute-start | bytes 393224 | tf_op jit(solution)/shard_map/ppermute | solution.py:254
  106.6 1.9 %collective-permute-start.14 = (f32[8,32,128]{2,1,0:T(8,128)S(1)}, f32[8,32,128]{2,1,0:T(8,128)S(1)}, u32[]{:S(2)}, u32[]{:S(2)}) collective-permute-start(f32[8,32,128]{2,1,0:T(8,128)S(1)} %get-tuple-element.53), channel_id=1, source_target_pairs={{0,6},{1,3},{2,0},{3,5},{4,2},{5,7},{6,4},{7,1},{8,14},{9,11},{10,... | collective-permute-start | bytes 393224 | tf_op jit(solution)/shard_map/ppermute | solution.py:254
  108.5 1.9 %collective-permute-start.11 = (f32[8,128]{1,0:T(8,128)S(1)}, f32[8,128]{1,0:T(8,128)S(1)}, u32[]{:S(2)}, u32[]{:S(2)}) collective-permute-start(f32[8,128]{1,0:T(8,128)S(1)} %get-tuple-element.49.checks), channel_id=1, source_target_pairs={{0,1},{1,0},{2,3},{3,2},{4,5},{5,4},{6,7},{7,6},{8,9},{9,8},{10,11... | collective-permute-start | bytes 12296 | tf_op jit(solution)/shard_map/ppermute | solution.py:227
  110.4 1.1 collective-permute-done.11.other_checks
  111.6 2.8 %collective-permute-done.14.refs_3_ = f32[8,32,128]{2,1,0:T(8,128)S(1)} collective-permute-done((f32[8,32,128]{2,1,0:T(8,128)S(1)}, f32[8,32,128]{2,1,0:T(8,128)S(1)}, u32[]{:S(2)}, u32[]{:S(2)}) %collective-permute-start.14) | collective-permute-done | bytes 131104 | tf_op jit(solution)/shard_map/ppermute | solution.py:254
  114.3 1.4 %shard_map.81 = (f32[32,4096]{1,0:T(8,128)}, f32[4,128]{1,0:T(4,128)}) custom-call(s32[5]{0:T(128)S(1)} %stack.23.place, f32[8,128]{1,0:T(8,128)S(1)} %get-tuple-element.49.checks, f32[8,128]{1,0:T(8,128)S(1)} %collective-permute-done.11.other_checks, f32[8,32,128]{2,1,0:T(8,128)S(1)} %get-tuple-element.50.refs_0_, ...), custom_call_target="tpu_custom_call" | custom-call | flops 1 | bytes 1 | tf_op jit(solution)/shard_map/pallas_call | solution.py:215
  (9 shorter events, 0.0 us)
Async XLA Ops:
  0.7 1.0 copy-start.1
  2.4 22.6 %collective-permute-start.1 = (f32[4,8,128,128]{3,2,1,0:T(8,128)}, f32[4,8,128,128]{3,2,1,0:T(8,128)S(1)}, u32[]{:S(2)}, u32[]{:S(2)}) collective-permute-start(f32[4,8,128,128]{3,2,1,0:T(8,128)} %own.1), channel_id=1, source_target_pairs={{0,1},{1,0},{2,3},{3,2},{4,5},{5,4},{6,7},{7,6},{8,9},{9,8},{10,11... | collective-permute-start | bytes 6291464 | tf_op jit(solution)/shard_map/ppermute | solution.py:227
  4.3 25.5 %collective-permute-start.2 = (f32[8,32,128]{2,1,0:T(8,128)S(1)}, f32[8,32,128]{2,1,0:T(8,128)S(1)}, u32[]{:S(2)}, u32[]{:S(2)}) collective-permute-start(f32[8,32,128]{2,1,0:T(8,128)S(1)} %get-tuple-element.35), channel_id=1, source_target_pairs={{0,2},{1,7},{2,4},{3,1},{4,6},{5,3},{6,0},{7,5},{8,10},{9,15},{10,... | collective-permute-start | bytes 393224 | tf_op jit(solution)/shard_map/ppermute | solution.py:254
  8.8 21.0 %collective-permute-start.3 = (f32[8,32,128]{2,1,0:T(8,128)S(1)}, f32[8,32,128]{2,1,0:T(8,128)S(1)}, u32[]{:S(2)}, u32[]{:S(2)}) collective-permute-start(f32[8,32,128]{2,1,0:T(8,128)S(1)} %get-tuple-element.36), channel_id=1, source_target_pairs={{0,4},{1,5},{2,6},{3,7},{4,0},{5,1},{6,2},{7,3},{8,12},{9,13},{10,... | collective-permute-start | bytes 393224 | tf_op jit(solution)/shard_map/ppermute | solution.py:254
  14.8 15.0 %collective-permute-start.4 = (f32[8,32,128]{2,1,0:T(8,128)S(1)}, f32[8,32,128]{2,1,0:T(8,128)S(1)}, u32[]{:S(2)}, u32[]{:S(2)}) collective-permute-start(f32[8,32,128]{2,1,0:T(8,128)S(1)} %get-tuple-element.37), channel_id=1, source_target_pairs={{0,6},{1,3},{2,0},{3,5},{4,2},{5,7},{6,4},{7,1},{8,14},{9,11},{10,... | collective-permute-start | bytes 393224 | tf_op jit(solution)/shard_map/ppermute | solution.py:254
  20.0 0.7 copy-start.2
  20.7 0.7 copy-start.3
  22.0 3.1 %collective-permute-start = (s32[4,128]{1,0:T(4,128)S(1)}, s32[4,128]{1,0:T(4,128)S(1)}, u32[]{:S(2)}, u32[]{:S(2)}) collective-permute-start(s32[4,128]{1,0:T(4,128)S(1)} %shard_map.69.ints_own), channel_id=1, source_target_pairs={{0,1},{1,0},{2,3},{3,2},{4,5},{5,4},{6,7},{7,6},{8,9},{9,8},{10,11... | collective-permute-start | bytes 6152 | tf_op jit(solution)/shard_map/ppermute | solution.py:227
  25.0 1.6 %copy-start = (f32[4,8,128,128]{3,2,1,0:T(8,128)S(1)}, f32[4,8,128,128]{3,2,1,0:T(8,128)}, u32[]{:S(2)}) copy-start(f32[4,8,128,128]{3,2,1,0:T(8,128)} %own.1) | copy-start | bytes 6291460
  30.6 20.5 %collective-permute-start.6 = (f32[520,128]{1,0:T(8,128)S(1)}, f32[520,128]{1,0:T(8,128)S(1)}, u32[]{:S(2)}, u32[]{:S(2)}) collective-permute-start(f32[520,128]{1,0:T(8,128)S(1)} %get-tuple-element.38.even.state.before), channel_id=1, source_target_pairs={{0,2},{1,511},{2,4},{3,1},{4,6},{5,3},{6,8},{7,5},{8,10},{9,7},{10... | collective-permute-start | bytes 798728 | tf_op jit(solution)/shard_map/ppermute | solution.py:260
  32.5 21.4 %collective-permute-start.5 = (f32[520,128]{1,0:T(8,128)S(1)}, f32[520,128]{1,0:T(8,128)S(1)}, u32[]{:S(2)}, u32[]{:S(2)}) collective-permute-start(f32[520,128]{1,0:T(8,128)S(1)} %get-tuple-element.39.odd.state.before), channel_id=1, source_target_pairs={{0,510},{1,3},{2,0},{3,5},{4,2},{5,7},{6,4},{7,9},{8,6},{9,11},{10... | collective-permute-start | bytes 798728 | tf_op jit(solution)/shard_map/ppermute | solution.py:260
  52.0 17.8 %collective-permute-start.7 = (f32[520,128]{1,0:T(8,128)S(1)}, f32[520,128]{1,0:T(8,128)S(1)}, u32[]{:S(2)}, u32[]{:S(2)}) collective-permute-start(f32[520,128]{1,0:T(8,128)S(1)} %shard_map.74.odd.state.before), channel_id=1, source_target_pairs={{0,510},{1,3},{2,0},{3,5},{4,2},{5,7},{6,4},{7,9},{8,6},{9,11},{10... | collective-permute-start | bytes 798728 | tf_op jit(solution)/shard_map/ppermute | solution.py:260
  54.9 17.8 %collective-permute-start.8 = (f32[520,128]{1,0:T(8,128)S(1)}, f32[520,128]{1,0:T(8,128)S(1)}, u32[]{:S(2)}, u32[]{:S(2)}) collective-permute-start(f32[520,128]{1,0:T(8,128)S(1)} %shard_map.73.even.state.before), channel_id=1, source_target_pairs={{0,2},{1,511},{2,4},{3,1},{4,6},{5,3},{6,8},{7,5},{8,10},{9,7},{10... | collective-permute-start | bytes 798728 | tf_op jit(solution)/shard_map/ppermute | solution.py:260
  70.8 14.3 %collective-permute-start.10 = (f32[520,128]{1,0:T(8,128)S(1)}, f32[520,128]{1,0:T(8,128)S(1)}, u32[]{:S(2)}, u32[]{:S(2)}) collective-permute-start(f32[520,128]{1,0:T(8,128)S(1)} %shard_map.76.even.state), channel_id=1, source_target_pairs={{0,2},{1,511},{2,4},{3,1},{4,6},{5,3},{6,8},{7,5},{8,10},{9,7},{10... | collective-permute-start | bytes 798728 | tf_op jit(solution)/shard_map/ppermute | solution.py:260
  73.7 17.6 %collective-permute-start.9 = (f32[520,128]{1,0:T(8,128)S(1)}, f32[520,128]{1,0:T(8,128)S(1)}, u32[]{:S(2)}, u32[]{:S(2)}) collective-permute-start(f32[520,128]{1,0:T(8,128)S(1)} %shard_map.77.odd.state), channel_id=1, source_target_pairs={{0,510},{1,3},{2,0},{3,5},{4,2},{5,7},{6,4},{7,9},{8,6},{9,11},{10... | collective-permute-start | bytes 798728 | tf_op jit(solution)/shard_map/ppermute | solution.py:260
  92.3 19.3 %collective-permute-start.12 = (f32[8,32,128]{2,1,0:T(8,128)S(1)}, f32[8,32,128]{2,1,0:T(8,128)S(1)}, u32[]{:S(2)}, u32[]{:S(2)}) collective-permute-start(f32[8,32,128]{2,1,0:T(8,128)S(1)} %get-tuple-element.51), channel_id=1, source_target_pairs={{0,2},{1,7},{2,4},{3,1},{4,6},{5,3},{6,0},{7,5},{8,10},{9,15},{10,... | collective-permute-start | bytes 393224 | tf_op jit(solution)/shard_map/ppermute | solution.py:254
  94.2 17.4 %collective-permute-start.13 = (f32[8,32,128]{2,1,0:T(8,128)S(1)}, f32[8,32,128]{2,1,0:T(8,128)S(1)}, u32[]{:S(2)}, u32[]{:S(2)}) collective-permute-start(f32[8,32,128]{2,1,0:T(8,128)S(1)} %get-tuple-element.52), channel_id=1, source_target_pairs={{0,4},{1,5},{2,6},{3,7},{4,0},{5,1},{6,2},{7,3},{8,12},{9,13},{10,... | collective-permute-start | bytes 393224 | tf_op jit(solution)/shard_map/ppermute | solution.py:254
  106.6 7.8 %collective-permute-start.14 = (f32[8,32,128]{2,1,0:T(8,128)S(1)}, f32[8,32,128]{2,1,0:T(8,128)S(1)}, u32[]{:S(2)}, u32[]{:S(2)}) collective-permute-start(f32[8,32,128]{2,1,0:T(8,128)S(1)} %get-tuple-element.53), channel_id=1, source_target_pairs={{0,6},{1,3},{2,0},{3,5},{4,2},{5,7},{6,4},{7,1},{8,14},{9,11},{10,... | collective-permute-start | bytes 393224 | tf_op jit(solution)/shard_map/ppermute | solution.py:254
  108.5 3.1 %collective-permute-start.11 = (f32[8,128]{1,0:T(8,128)S(1)}, f32[8,128]{1,0:T(8,128)S(1)}, u32[]{:S(2)}, u32[]{:S(2)}) collective-permute-start(f32[8,128]{1,0:T(8,128)S(1)} %get-tuple-element.49.checks), channel_id=1, source_target_pairs={{0,1},{1,0},{2,3},{3,2},{4,5},{5,4},{6,7},{7,6},{8,9},{9,8},{10,11... | collective-permute-start | bytes 12296 | tf_op jit(solution)/shard_map/ppermute | solution.py:227

commit v3 on v2

--- a/solution.py
+++ b/solution.py
@@ -19,6 +19,8 @@
 
 VMEM = pl.BlockSpec(memory_space=pltpu.VMEM)
 SMEM = pl.BlockSpec(memory_space=pltpu.SMEM)
+ANY = pl.BlockSpec(memory_space=pl.ANY)
+HBM = pl.BlockSpec(memory_space=pltpu.HBM)
 
 
 def split(value):
@@ -27,15 +29,24 @@
     return high, low
 
 
-def prepare_kernel(total, place, ints_own, ints_other, own, other, rhs, near_list, even_list, odd_list):
+def prepare_kernel(
+    total, place, ints_own, ints_other, source, other, rhs, near_list, even_list, odd_list, own, semaphores
+):
     rows, cap = own.shape[0], own.shape[1]
+    copies = [
+        pltpu.make_async_copy(source.at[row], own.at[row], semaphores.at[row]) for row in range(rows)
+    ]
+    for copy in copies:
+        copy.start()
     core, base, swap = place[0], place[1], place[3]
     chip_rows = CORES * rows
     rhs[chip_rows * cap] = jnp.zeros(rhs.shape[1:], rhs.dtype)
     lists = (near_list, even_list, odd_list)
     used = (jnp.int32(0),) * 3
-    for ints, blocks, side in ((ints_own, own, core), (ints_other, other, 1 - core)):
+    for ints, blocks, side in ((ints_other, other, 1 - core), (ints_own, own, core)):
         for row in range(rows):
+            if blocks is own:
+                copies[row].wait()
             chip_row = side * rows + row
 
             def one(slot, used, ints=ints, blocks=blocks, row=row, chip_row=chip_row):
@@ -67,7 +78,7 @@
                     following.append(count + chosen.astype(jnp.int32))
                 return tuple(following)
 
-            used = lax.fori_loop(0, ints[row, cap], one, used)
+            used = lax.fori_loop(0, ints[rows, row], one, used)
     for entries, count in zip(lists, used):
         for extra in range(GROUP - 1):
             entries[0, count + extra] = 0
@@ -109,9 +120,12 @@
     lax.fori_loop(0, entries[3, 0], group, 0)
 
 
-def near_kernel(even, odd, entries, rhs, even_total, odd_total, halves, total):
+def near_kernel(even, odd, listed, rhs, even_total, odd_total, halves, total, entries, semaphore):
+    copy = pltpu.make_async_copy(listed, entries, semaphore)
+    copy.start()
     total[...] = jnp.zeros(total.shape, total.dtype)
     stage([even, odd], halves)
+    copy.wait()
     multiply(entries, rhs, halves, total)
     even_total[...] = total[:REACH]
     odd_total[...] = total[REACH:]
@@ -129,27 +143,41 @@
     return pair
 
 
-def far_kernel(first, state, before, near_total, halo, entries, rhs, out, halves, total):
-    width = halves.shape[1] - 16
+def far_products(near_total, halo, listed, rhs, halves, total, entries, semaphore):
+    copy = pltpu.make_async_copy(listed, entries, semaphore)
+    copy.start()
     total[...] = near_total[...]
     stage([halo], halves)
+    copy.wait()
     multiply(entries, rhs, halves, total)
+    return halves.shape[1] - 16
+
+
+def far_kernel(first, state, before, near_total, halo, listed, rhs, out, halves, total, *lists):
+    width = far_products(near_total, halo, listed, rhs, halves, total, *lists)
     for tile in range(REACH):
         main, row = update(first, tile, state, before, total, width)
         out[tile * width : (tile + 1) * width, :] = main
         out[REACH * width + tile : REACH * width + tile + 1, :] = row
 
 
-def last_kernel(place, state, before, near_total, halo, entries, rhs, odd, *refs):
-    halves, total, keep = refs[-3:]
-    outs, checks = refs[:-4], refs[-4]
+def swap_here():
+    return REACH * (1 - lax.axis_index("core"))
+
+
+def part_from(steps):
+    parts = lax.axis_size("part")
+    return lax.rem(lax.axis_index("part") + steps * (1 - 2 * lax.axis_index("core")) + parts, parts)
+
+
+def last_kernel(state, before, near_total, halo, listed, rhs, odd, *refs):
+    halves, total, entries, semaphore, keep = refs[-5:]
+    outs, checks = refs[:-6], refs[-6]
     parts = len(outs)
-    width = halves.shape[1] - 16
+    width = far_products(near_total, halo, listed, rhs, halves, total, entries, semaphore)
     each = width // parts
-    total[...] = near_total[...]
-    stage([halo], halves)
-    multiply(entries, rhs, halves, total)
-    even_at, odd_at = place[3], REACH - place[3]
+    swap = swap_here()
+    even_at, odd_at = swap, REACH - swap
     for tile in range(REACH):
         main, row = update(False, tile, state, before, total, width)
         keep[tile * width : (tile + 1) * width, :] = main
@@ -157,22 +185,23 @@
         spot = REACH * width + tile
         checks[pl.ds(odd_at + tile, 1), :] = odd[spot : spot + 1, :]
     for steps, out in enumerate(outs):
-        at = pl.multiple_of(lax.rem(place[2] + steps * place[4] + parts, parts) * each, each)
+        at = pl.multiple_of(part_from(steps) * each, each)
         for tile in range(REACH):
             out[even_at + tile] = keep[pl.ds(tile * width + at, each), :]
             out[odd_at + tile] = odd[pl.ds(tile * width + at, each), :]
 
 
-def gather_kernel(place, weights, *refs):
+def gather_kernel(order, weights, *refs):
+    del order
     parts = weights.shape[0] // refs[0].shape[1]
     pieces, halves = refs[:parts], refs[parts:]
     each = pieces[0].shape[1]
     width = parts * each
-    for half, start in zip(halves, (place[3], REACH - place[3])):
+    for half, start in zip(halves, (swap_here(), REACH - swap_here())):
         for tile in range(REACH):
             row = jnp.zeros((1, B), jnp.float32)
             for steps, piece in enumerate(pieces):
-                at = pl.multiple_of(lax.rem(place[2] - steps * place[4] + parts, parts) * each, each)
+                at = pl.multiple_of(part_from(-steps) * each, each)
                 value = piece[start + tile]
                 row = row + jnp.sum(value * weights[pl.ds(at, each), :], axis=0, keepdims=True)
                 half[pl.ds(tile * width + at, each), :] = value
@@ -180,34 +209,34 @@
             half[spot : spot + 1, :] = row
 
 
-def arrange_kernel(place, vectors, *pieces):
+def arrange_kernel(vectors, *refs):
+    pieces, semaphores = refs[:-1], refs[-1]
     parts, tiles = len(pieces), pieces[0].shape[0]
-    for steps, ref in enumerate(pieces):
-        at = lax.rem(place[2] + steps * place[4] + parts, parts) * (tiles * B)
+    copies = []
+    for steps in (*range(1, parts), 0):
+        at = part_from(steps) * (tiles * B)
         for tile in range(tiles):
-            ref[tile] = vectors[:, pl.ds(pl.multiple_of(at + tile * B, B), B)]
-
-
-def integers_kernel(cols, counts, ints):
-    rows, cap = cols.shape
-    lane = lax.broadcasted_iota(jnp.int32, (1, B), 1)
-    for row in range(rows):
-        value = jnp.where(lane == cap, counts[row], 0)
-        for slot in range(cap):
-            value = jnp.where(lane == slot, cols[row, slot], value)
-        ints[row : row + 1, :] = value
-
-
-def place_kernel(place, checks, other_checks, *refs):
+            lanes = pl.ds(pl.multiple_of(at + tile * B, B), B)
+            semaphore = semaphores.at[steps * tiles + tile]
+            copies.append(
+                pltpu.make_async_copy(vectors.at[:, lanes], pieces[steps].at[tile], semaphore)
+            )
+    for copy in copies:
+        copy.start()
+    for copy in copies:
+        copy.wait()
+
+
+def place_kernel(checks, other_checks, *refs):
     pieces, (out, out_check) = refs[:-2], refs[-2:]
     parts, tiles = len(pieces), pieces[0].shape[0]
     for steps, piece in enumerate(pieces):
-        at = lax.rem(place[2] - steps * place[4] + parts, parts) * (tiles * B)
+        at = part_from(-steps) * (tiles * B)
         for tile in range(tiles):
             out[:, pl.ds(pl.multiple_of(at + tile * B, B), B)] = piece[tile]
     rows = out_check.shape[0]
     for row in range(rows):
-        line = pl.ds(place[0] * rows + row, 1)
+        line = pl.ds(lax.axis_index("core") * rows + row, 1)
         out_check[row : row + 1, :] = checks[line, :] + other_checks[line, :]
 
 
@@ -240,7 +269,7 @@
     width = parts * each
 
     swap = REACH * (1 - core)
-    place = jnp.stack([core, chip * tiles, lax.axis_index("part"), swap, 1 - 2 * core]).astype(jnp.int32)
+    place = jnp.stack([core, chip * tiles, lax.axis_index("part"), swap]).astype(jnp.int32)
 
     def pairs(count, steps):
         return [
@@ -260,37 +289,37 @@
         return lax.ppermute(value, ("row", "part", "core"), pairs(chips, steps))
 
     piece = ((tiles, each, B), f32, VMEM)
-    sent = call(arrange_kernel, (piece,) * parts, [(place, SMEM), (start_vectors.T, VMEM)])
+    copies = pltpu.SemaphoreType.DMA((parts * tiles,))
+    sent = call(arrange_kernel, (piece,) * parts, [(pltpu.with_memory_space_constraint(start_vectors.T, pltpu.HBM), HBM)], [copies])
     arrived = exchange(sent)
     blocks, columns, counts, _ = lax.optimization_barrier(
         (ham_blocks, block_cols, block_counts, sent[0])
     )
-    (ints,) = call(
-        integers_kernel, (((rows, B), jnp.int32, VMEM),), [(columns, SMEM), (counts, SMEM)]
-    )
+    ints = jnp.concatenate([columns, jnp.pad(counts, (0, cap - rows))[None, :]], 0)
     other_ints = shift(ints, "core", CORES, 1)
     other_blocks = shift(blocks, "core", CORES, 1)
     list_shape = ((4, tiles * cap + GROUP), jnp.int32, SMEM)
     rhs, near_list, even_list, odd_list = call(
         functools.partial(prepare_kernel, total),
         (((tiles * cap + 1, B, 2 * B), jnp.bfloat16, VMEM), list_shape, list_shape, list_shape),
-        [(place, SMEM), (ints, SMEM), (other_ints, SMEM), (ham_blocks, VMEM), (other_blocks, VMEM)],
+        [(place, SMEM), (ints, SMEM), (other_ints, SMEM), (pltpu.with_memory_space_constraint(ham_blocks, pltpu.HBM), HBM), (other_blocks, VMEM)],
+        [pltpu.VMEM(ham_blocks.shape, f32), pltpu.SemaphoreType.DMA((rows,))],
     )
     mine = lax.dynamic_index_in_dim(check_weights.reshape(parts, CORES, each), core, 1, False)
     weights = jnp.broadcast_to(mine.reshape(width, 1), (width, B))
     full = ((REACH * width + CHECK, B), f32, VMEM)
-    placed, _ = lax.optimization_barrier((place, near_list))
     even, odd = call(
         gather_kernel,
         (full, full),
-        [(placed, SMEM), (weights, VMEM)] + [(value, VMEM) for value in arrived],
+        [(near_list, ANY), (weights, VMEM)] + [(value, VMEM) for value in arrived],
     )
     even_before, odd_before = even, odd
+    list_scratch = [pltpu.SMEM(list_shape[0], jnp.int32), pltpu.SemaphoreType.DMA(())]
     part_total = ((REACH, width + 16, B), f32, VMEM)
     scratch = [
         pltpu.VMEM((REACH, width + 16, 2 * B), jnp.bfloat16),
         pltpu.VMEM((REACH, width + 16, B), f32),
-    ]
+    ] + list_scratch
     for step in range(ITERS):
         first, last = step == 0, step == ITERS - 1
         odd_halo = round_chips(even, 1)
@@ -298,16 +327,17 @@
         even_total, odd_total = call(
             near_kernel,
             (part_total, part_total),
-            [(even, VMEM), (odd, VMEM), (near_list, SMEM), (rhs, VMEM)],
+            [(even, VMEM), (odd, VMEM), (near_list, ANY), (rhs, VMEM)],
             [
                 pltpu.VMEM((tiles, width + 16, 2 * B), jnp.bfloat16),
                 pltpu.VMEM((tiles, width + 16, B), f32),
-            ],
+            ]
+            + list_scratch,
         )
 
         def inputs(state, before, near_total, halo, entries):
             values = (state, before, near_total, halo)
-            return [(value, VMEM) for value in values] + [(entries, SMEM), (rhs, VMEM)]
+            return [(value, VMEM) for value in values] + [(entries, ANY), (rhs, VMEM)]
 
         kernel = functools.partial(far_kernel, first)
         (odd_next,) = call(
@@ -318,7 +348,7 @@
             *outs, checks = call(
                 last_kernel,
                 (piece,) * parts + (((tiles, B), f32, VMEM),),
-                [(place, SMEM)] + even_inputs + [(odd_next, VMEM)],
+                even_inputs + [(odd_next, VMEM)],
                 scratch + [pltpu.VMEM((REACH * width, B), f32)],
             )
             break
@@ -329,7 +359,7 @@
     filtered, check_sums = call(
         place_kernel,
         (((each, parts * tiles * B), f32, VMEM), ((rows, B), f32, VMEM)),
-        [(place, SMEM), (checks, VMEM), (shift(checks, "core", CORES, 1), VMEM)]
+        [(checks, VMEM), (shift(checks, "core", CORES, 1), VMEM)]
         + [(value, VMEM) for value in returned],
     )
     return filtered.T, check_sums.reshape(rows * B)

time: 116 us -> 117 us (level)
  the two profiles are of different devices: /device:TPU:448 before, /device:TPU:206 now
where the time goes in v3:
time: 117 us; the launch traced here: 116 us
  starting transfers between devices  70.5 us (60%)
  waiting for transfers between devices  26.2 us (22%)
  Pallas kernels  16 us (14%)
  local copies, waits for them, and re-layouts  1.6 us (1%)
    ppermute x6, starting transfers between devices, exchange(): lax.ppermute(pieces[steps], ('part', 'core'), pairs(parts, steps))  40.3 us
    ppermute x6, starting transfers between devices, round_chips(): return lax.ppermute(value, ('row', 'part', 'core'), pairs(chips, steps))  24.4 us
    ppermute x6, waiting for transfers between devices, round_chips(): return lax.ppermute(value, ('row', 'part', 'core'), pairs(chips, steps))  22.1 us
    pallas_call x13, Pallas kernels, call(): pl.pallas_call(kernel, out_shape=tuple((jax.ShapeDtypeStruct(shape, dtype...  16 us
    ppermute x3, starting transfers between devices, shift(): lax.ppermute(value, axes, [(at, (at + steps) % count) for at in range(cou...  5.75 us
    ppermute x6, waiting for transfers between devices, exchange(): lax.ppermute(pieces[steps], ('part', 'core'), pairs(parts, steps))  2.78 us
  transfers between devices with their start and end apart: 15, of which 7 were waited for; matrix products, arithmetic and copies ran while one was open for 2% of the time, Pallas kernels for 11%

profile of v3, /device:TPU:206, one launch (start us, length us, event | category | flops | bytes accessed | tf_op | source)
XLA Modules:
  0.0 115.9 jit_solution(12037886786862923636)
XLA Ops:
  0.6 1.3 %shard_map.68 = (f32[8,32,128]{2,1,0:T(8,128)S(1)}, f32[8,32,128]{2,1,0:T(8,128)S(1)}, f32[8,32,128]{2,1,0:T(8,128)S(1)}, f32[8,32,128]{2,1,0:T(8,128)S(1)}) custom-call(f32[32,4096]{1,0:T(8,128)} %bitcast.9), custom_call_target="tpu_custom_call" | custom-call | flops 1 | bytes 1 | tf_op jit(solution)/shard_map/pallas_call | solution.py:244
  1.9 1.9 %collective-permute-start.1 = (f32[4,8,128,128]{3,2,1,0:T(8,128)}, f32[4,8,128,128]{3,2,1,0:T(8,128)S(1)}, u32[]{:S(2)}, u32[]{:S(2)}) collective-permute-start(f32[4,8,128,128]{3,2,1,0:T(8,128)} %source.1), channel_id=1, source_target_pairs={{0,1},{1,0},{2,3},{3,2},{4,5},{5,4},{6,7},{7,6},{8,9},{9,8},{10,11... | collective-permute-start | bytes 6291464 | tf_op jit(solution)/shard_map/ppermute | solution.py:256
  3.9 4.5 %collective-permute-start.2 = (f32[8,32,128]{2,1,0:T(8,128)S(1)}, f32[8,32,128]{2,1,0:T(8,128)S(1)}, u32[]{:S(2)}, u32[]{:S(2)}) collective-permute-start(f32[8,32,128]{2,1,0:T(8,128)S(1)} %get-tuple-element.33), channel_id=1, source_target_pairs={{0,2},{1,7},{2,4},{3,1},{4,6},{5,3},{6,0},{7,5},{8,10},{9,15},{10,... | collective-permute-start | bytes 393224 | tf_op jit(solution)/shard_map/ppermute | solution.py:283
  8.4 5.0 %collective-permute-start.3 = (f32[8,32,128]{2,1,0:T(8,128)S(1)}, f32[8,32,128]{2,1,0:T(8,128)S(1)}, u32[]{:S(2)}, u32[]{:S(2)}) collective-permute-start(f32[8,32,128]{2,1,0:T(8,128)S(1)} %get-tuple-element.34), channel_id=1, source_target_pairs={{0,4},{1,5},{2,6},{3,7},{4,0},{5,1},{6,2},{7,3},{8,12},{9,13},{10,... | collective-permute-start | bytes 393224 | tf_op jit(solution)/shard_map/ppermute | solution.py:283
  13.4 5.3 %collective-permute-start.4 = (f32[8,32,128]{2,1,0:T(8,128)S(1)}, f32[8,32,128]{2,1,0:T(8,128)S(1)}, u32[]{:S(2)}, u32[]{:S(2)}) collective-permute-start(f32[8,32,128]{2,1,0:T(8,128)S(1)} %get-tuple-element.35), channel_id=1, source_target_pairs={{0,6},{1,3},{2,0},{3,5},{4,2},{5,7},{6,4},{7,1},{8,14},{9,11},{10,... | collective-permute-start | bytes 393224 | tf_op jit(solution)/shard_map/ppermute | solution.py:283
  18.7 0.7 pad_bitcast_fusion
  19.3 0.7 pad_add_fusion.ints_own
  20.0 1.9 %collective-permute-start = (s32[5,8]{1,0:T(8,128)S(1)}, s32[5,8]{1,0:T(8,128)S(1)}, u32[]{:S(2)}, u32[]{:S(2)}) collective-permute-start(s32[5,8]{1,0:T(8,128)S(1)} %pad_add_fusion.ints_own), channel_id=1, source_target_pairs={{0,1},{1,0},{2,3},{3,2},{4,5},{5,4},{6,7},{7,6},{8,9},{9,8},{10,11... | collective-permute-start | bytes 488 | tf_op jit(solution)/shard_map/ppermute | solution.py:256
  22.0 0.8 reshape.13
  22.7 0.1 pad_add_fusion.1.place
  22.8 0.1 broadcast_in_dim.11
  22.9 0.2 collective-permute-done.ints_other
  23.1 0.0 collective-permute-done.1.other
  23.1 3.3 %shard_map.69 = (bf16[65,128,256]{2,1,0:T(8,128)(2,1)S(1)}, s32[4,68]{1,0:T(4,128)S(1)}, s32[4,68]{1,0:T(4,128)S(1)}, s32[4,68]{1,0:T(4,128)S(1)}) custom-call(s32[4]{0:T(128)S(1)} %pad_add_fusion.1.place, s32[5,8]{1,0:T(8,128)S(1)} %pad_add_fusion.ints_own, s32[5,8]{1,0:T(8,128)S(1)} %collective-permute-done.ints_other, f32[4,8,128,128]{3,2,1,0:T(8,128)} %source.1, ...), custom_call_target="tpu_custom_call" | custom-call | flops 1 | bytes 1 | tf_op jit(solution)/shard_map/pallas_call | solution.py:244
  26.4 0.0 collective-permute-done.2.refs_1_
  26.4 0.0 collective-permute-done.3.refs_2_
  26.4 0.0 collective-permute-done.4.refs_3_
  26.5 0.1 broadcast_in_dim.12.weights
  26.5 0.1 shard_map.70
  26.6 2.1 %collective-permute-start.6 = (f32[520,128]{1,0:T(8,128)S(1)}, f32[520,128]{1,0:T(8,128)S(1)}, u32[]{:S(2)}, u32[]{:S(2)}) collective-permute-start(f32[520,128]{1,0:T(8,128)S(1)} %get-tuple-element.36.even.state.before), channel_id=1, source_target_pairs={{0,2},{1,511},{2,4},{3,1},{4,6},{5,3},{6,8},{7,5},{8,10},{9,7},{10... | collective-permute-start | bytes 798728 | tf_op jit(solution)/shard_map/ppermute | solution.py:289
  28.8 6.7 %collective-permute-start.5 = (f32[520,128]{1,0:T(8,128)S(1)}, f32[520,128]{1,0:T(8,128)S(1)}, u32[]{:S(2)}, u32[]{:S(2)}) collective-permute-start(f32[520,128]{1,0:T(8,128)S(1)} %get-tuple-element.37.odd.state.before), channel_id=1, source_target_pairs={{0,510},{1,3},{2,0},{3,5},{4,2},{5,7},{6,4},{7,9},{8,6},{9,11},{10... | collective-permute-start | bytes 798728 | tf_op jit(solution)/shard_map/ppermute | solution.py:289
  35.5 1.6 %shard_map.71 = (f32[4,144,128]{2,1,0:T(8,128)S(1)}, f32[4,144,128]{2,1,0:T(8,128)S(1)}) custom-call(f32[520,128]{1,0:T(8,128)S(1)} %get-tuple-element.36.even.state.before, f32[520,128]{1,0:T(8,128)S(1)} %get-tuple-element.37.odd.state.before, s32[4,68]{1,0:T(4,128)S(1)} %get-tuple-element.32.order.listed, bf16[65,128,256]{2,1,0:T(8,128)(2,1)S(1)} %get-tuple-element.38.rhs), custom_call_target="tpu_custom_call" | custom-call | flops 1 | bytes 1 | tf_op jit(solution)/shard_map/pallas_call | solution.py:244
  37.1 4.7 %collective-permute-done.6.halo = f32[520,128]{1,0:T(8,128)S(1)} collective-permute-done((f32[520,128]{1,0:T(8,128)S(1)}, f32[520,128]{1,0:T(8,128)S(1)}, u32[]{:S(2)}, u32[]{:S(2)}) %collective-permute-start.6) | collective-permute-done | bytes 266272 | tf_op jit(solution)/shard_map/ppermute | solution.py:289
  41.9 0.9 shard_map.73.odd.state.before
  42.8 1.9 %collective-permute-start.7 = (f32[520,128]{1,0:T(8,128)S(1)}, f32[520,128]{1,0:T(8,128)S(1)}, u32[]{:S(2)}, u32[]{:S(2)}) collective-permute-start(f32[520,128]{1,0:T(8,128)S(1)} %shard_map.73.odd.state.before), channel_id=1, source_target_pairs={{0,510},{1,3},{2,0},{3,5},{4,2},{5,7},{6,4},{7,9},{8,6},{9,11},{10... | collective-permute-start | bytes 798728 | tf_op jit(solution)/shard_map/ppermute | solution.py:289
  44.7 0.0 collective-permute-done.5.halo
  44.7 0.9 shard_map.72.even.state.before
  45.6 4.8 %collective-permute-start.8 = (f32[520,128]{1,0:T(8,128)S(1)}, f32[520,128]{1,0:T(8,128)S(1)}, u32[]{:S(2)}, u32[]{:S(2)}) collective-permute-start(f32[520,128]{1,0:T(8,128)S(1)} %shard_map.72.even.state.before), channel_id=1, source_target_pairs={{0,2},{1,511},{2,4},{3,1},{4,6},{5,3},{6,8},{7,5},{8,10},{9,7},{10... | collective-permute-start | bytes 798728 | tf_op jit(solution)/shard_map/ppermute | solution.py:289
  50.4 1.6 %shard_map.74 = (f32[4,144,128]{2,1,0:T(8,128)S(1)}, f32[4,144,128]{2,1,0:T(8,128)S(1)}) custom-call(f32[520,128]{1,0:T(8,128)S(1)} %shard_map.72.even.state.before, f32[520,128]{1,0:T(8,128)S(1)} %shard_map.73.odd.state.before, s32[4,68]{1,0:T(4,128)S(1)} %get-tuple-element.32.order.listed, bf16[65,128,256]{2,1,0:T(8,128)(2,1)S(1)} %get-tuple-element.38.rhs), custom_call_target="tpu_custom_call" | custom-call | flops 1 | bytes 1 | tf_op jit(solution)/shard_map/pallas_call | solution.py:244
  52.1 6.0 %collective-permute-done.7.halo = f32[520,128]{1,0:T(8,128)S(1)} collective-permute-done((f32[520,128]{1,0:T(8,128)S(1)}, f32[520,128]{1,0:T(8,128)S(1)}, u32[]{:S(2)}, u32[]{:S(2)}) %collective-permute-start.7) | collective-permute-done | bytes 266272 | tf_op jit(solution)/shard_map/ppermute | solution.py:289
  58.1 0.9 shard_map.75.even.state
  59.0 6.8 %collective-permute-start.10 = (f32[520,128]{1,0:T(8,128)S(1)}, f32[520,128]{1,0:T(8,128)S(1)}, u32[]{:S(2)}, u32[]{:S(2)}) collective-permute-start(f32[520,128]{1,0:T(8,128)S(1)} %shard_map.75.even.state), channel_id=1, source_target_pairs={{0,2},{1,511},{2,4},{3,1},{4,6},{5,3},{6,8},{7,5},{8,10},{9,7},{10... | collective-permute-start | bytes 798728 | tf_op jit(solution)/shard_map/ppermute | solution.py:289
  65.9 0.0 collective-permute-done.8.halo
  65.9 0.9 shard_map.76.odd.state
  66.8 2.0 %collective-permute-start.9 = (f32[520,128]{1,0:T(8,128)S(1)}, f32[520,128]{1,0:T(8,128)S(1)}, u32[]{:S(2)}, u32[]{:S(2)}) collective-permute-start(f32[520,128]{1,0:T(8,128)S(1)} %shard_map.76.odd.state), channel_id=1, source_target_pairs={{0,510},{1,3},{2,0},{3,5},{4,2},{5,7},{6,4},{7,9},{8,6},{9,11},{10... | collective-permute-start | bytes 798728 | tf_op jit(solution)/shard_map/ppermute | solution.py:289
  68.8 1.6 %shard_map.77 = (f32[4,144,128]{2,1,0:T(8,128)S(1)}, f32[4,144,128]{2,1,0:T(8,128)S(1)}) custom-call(f32[520,128]{1,0:T(8,128)S(1)} %shard_map.75.even.state, f32[520,128]{1,0:T(8,128)S(1)} %shard_map.76.odd.state, s32[4,68]{1,0:T(4,128)S(1)} %get-tuple-element.32.order.listed, bf16[65,128,256]{2,1,0:T(8,128)(2,1)S(1)} %get-tuple-element.38.rhs), custom_call_target="tpu_custom_call" | custom-call | flops 1 | bytes 1 | tf_op jit(solution)/shard_map/pallas_call | solution.py:244
  70.5 2.6 %collective-permute-done.10.halo = f32[520,128]{1,0:T(8,128)S(1)} collective-permute-done((f32[520,128]{1,0:T(8,128)S(1)}, f32[520,128]{1,0:T(8,128)S(1)}, u32[]{:S(2)}, u32[]{:S(2)}) %collective-permute-start.10) | collective-permute-done | bytes 266272 | tf_op jit(solution)/shard_map/ppermute | solution.py:289
  73.1 0.9 shard_map.78.odd
  74.0 8.7 %collective-permute-done.9.halo = f32[520,128]{1,0:T(8,128)S(1)} collective-permute-done((f32[520,128]{1,0:T(8,128)S(1)}, f32[520,128]{1,0:T(8,128)S(1)}, u32[]{:S(2)}, u32[]{:S(2)}) %collective-permute-start.9) | collective-permute-done | bytes 266272 | tf_op jit(solution)/shard_map/ppermute | solution.py:289
  82.7 0.9 shard_map.79
  83.7 5.6 %collective-permute-start.12 = (f32[8,32,128]{2,1,0:T(8,128)S(1)}, f32[8,32,128]{2,1,0:T(8,128)S(1)}, u32[]{:S(2)}, u32[]{:S(2)}) collective-permute-start(f32[8,32,128]{2,1,0:T(8,128)S(1)} %get-tuple-element.49), channel_id=1, source_target_pairs={{0,2},{1,7},{2,4},{3,1},{4,6},{5,3},{6,0},{7,5},{8,10},{9,15},{10,... | collective-permute-start | bytes 393224 | tf_op jit(solution)/shard_map/ppermute | solution.py:283
  89.3 18.0 %collective-permute-start.13 = (f32[8,32,128]{2,1,0:T(8,128)S(1)}, f32[8,32,128]{2,1,0:T(8,128)S(1)}, u32[]{:S(2)}, u32[]{:S(2)}) collective-permute-start(f32[8,32,128]{2,1,0:T(8,128)S(1)} %get-tuple-element.50), channel_id=1, source_target_pairs={{0,4},{1,5},{2,6},{3,7},{4,0},{5,1},{6,2},{7,3},{8,12},{9,13},{10,... | collective-permute-start | bytes 393224 | tf_op jit(solution)/shard_map/ppermute | solution.py:283
  107.3 1.9 %collective-permute-start.14 = (f32[8,32,128]{2,1,0:T(8,128)S(1)}, f32[8,32,128]{2,1,0:T(8,128)S(1)}, u32[]{:S(2)}, u32[]{:S(2)}) collective-permute-start(f32[8,32,128]{2,1,0:T(8,128)S(1)} %get-tuple-element.51), channel_id=1, source_target_pairs={{0,6},{1,3},{2,0},{3,5},{4,2},{5,7},{6,4},{7,1},{8,14},{9,11},{10,... | collective-permute-start | bytes 393224 | tf_op jit(solution)/shard_map/ppermute | solution.py:283
  109.2 1.9 %collective-permute-start.11 = (f32[8,128]{1,0:T(8,128)S(1)}, f32[8,128]{1,0:T(8,128)S(1)}, u32[]{:S(2)}, u32[]{:S(2)}) collective-permute-start(f32[8,128]{1,0:T(8,128)S(1)} %get-tuple-element.47.checks), channel_id=1, source_target_pairs={{0,1},{1,0},{2,3},{3,2},{4,5},{5,4},{6,7},{7,6},{8,9},{9,8},{10,11... | collective-permute-start | bytes 12296 | tf_op jit(solution)/shard_map/ppermute | solution.py:256
  111.1 1.1 collective-permute-done.11.other_checks
  112.3 0.0 collective-permute-done.13.refs_2_
  112.3 2.8 %collective-permute-done.14.refs_3_ = f32[8,32,128]{2,1,0:T(8,128)S(1)} collective-permute-done((f32[8,32,128]{2,1,0:T(8,128)S(1)}, f32[8,32,128]{2,1,0:T(8,128)S(1)}, u32[]{:S(2)}, u32[]{:S(2)}) %collective-permute-start.14) | collective-permute-done | bytes 131104 | tf_op jit(solution)/shard_map/ppermute | solution.py:283
  115.0 0.9 shard_map.80
  (2 shorter events, 0.0 us)
Async XLA Ops:
  1.9 21.1 %collective-permute-start.1 = (f32[4,8,128,128]{3,2,1,0:T(8,128)}, f32[4,8,128,128]{3,2,1,0:T(8,128)S(1)}, u32[]{:S(2)}, u32[]{:S(2)}) collective-permute-start(f32[4,8,128,128]{3,2,1,0:T(8,128)} %source.1), channel_id=1, source_target_pairs={{0,1},{1,0},{2,3},{3,2},{4,5},{5,4},{6,7},{7,6},{8,9},{9,8},{10,11... | collective-permute-start | bytes 6291464 | tf_op jit(solution)/shard_map/ppermute | solution.py:256
  3.9 22.6 %collective-permute-start.2 = (f32[8,32,128]{2,1,0:T(8,128)S(1)}, f32[8,32,128]{2,1,0:T(8,128)S(1)}, u32[]{:S(2)}, u32[]{:S(2)}) collective-permute-start(f32[8,32,128]{2,1,0:T(8,128)S(1)} %get-tuple-element.33), channel_id=1, source_target_pairs={{0,2},{1,7},{2,4},{3,1},{4,6},{5,3},{6,0},{7,5},{8,10},{9,15},{10,... | collective-permute-start | bytes 393224 | tf_op jit(solution)/shard_map/ppermute | solution.py:283
  8.4 18.1 %collective-permute-start.3 = (f32[8,32,128]{2,1,0:T(8,128)S(1)}, f32[8,32,128]{2,1,0:T(8,128)S(1)}, u32[]{:S(2)}, u32[]{:S(2)}) collective-permute-start(f32[8,32,128]{2,1,0:T(8,128)S(1)} %get-tuple-element.34), channel_id=1, source_target_pairs={{0,4},{1,5},{2,6},{3,7},{4,0},{5,1},{6,2},{7,3},{8,12},{9,13},{10,... | collective-permute-start | bytes 393224 | tf_op jit(solution)/shard_map/ppermute | solution.py:283
  13.4 13.0 %collective-permute-start.4 = (f32[8,32,128]{2,1,0:T(8,128)S(1)}, f32[8,32,128]{2,1,0:T(8,128)S(1)}, u32[]{:S(2)}, u32[]{:S(2)}) collective-permute-start(f32[8,32,128]{2,1,0:T(8,128)S(1)} %get-tuple-element.35), channel_id=1, source_target_pairs={{0,6},{1,3},{2,0},{3,5},{4,2},{5,7},{6,4},{7,1},{8,14},{9,11},{10,... | collective-permute-start | bytes 393224 | tf_op jit(solution)/shard_map/ppermute | solution.py:283
  20.0 3.0 %collective-permute-start = (s32[5,8]{1,0:T(8,128)S(1)}, s32[5,8]{1,0:T(8,128)S(1)}, u32[]{:S(2)}, u32[]{:S(2)}) collective-permute-start(s32[5,8]{1,0:T(8,128)S(1)} %pad_add_fusion.ints_own), channel_id=1, source_target_pairs={{0,1},{1,0},{2,3},{3,2},{4,5},{5,4},{6,7},{7,6},{8,9},{9,8},{10,11... | collective-permute-start | bytes 488 | tf_op jit(solution)/shard_map/ppermute | solution.py:256
  26.6 15.3 %collective-permute-start.6 = (f32[520,128]{1,0:T(8,128)S(1)}, f32[520,128]{1,0:T(8,128)S(1)}, u32[]{:S(2)}, u32[]{:S(2)}) collective-permute-start(f32[520,128]{1,0:T(8,128)S(1)} %get-tuple-element.36.even.state.before), channel_id=1, source_target_pairs={{0,2},{1,511},{2,4},{3,1},{4,6},{5,3},{6,8},{7,5},{8,10},{9,7},{10... | collective-permute-start | bytes 798728 | tf_op jit(solution)/shard_map/ppermute | solution.py:289
  28.8 15.9 %collective-permute-start.5 = (f32[520,128]{1,0:T(8,128)S(1)}, f32[520,128]{1,0:T(8,128)S(1)}, u32[]{:S(2)}, u32[]{:S(2)}) collective-permute-start(f32[520,128]{1,0:T(8,128)S(1)} %get-tuple-element.37.odd.state.before), channel_id=1, source_target_pairs={{0,510},{1,3},{2,0},{3,5},{4,2},{5,7},{6,4},{7,9},{8,6},{9,11},{10... | collective-permute-start | bytes 798728 | tf_op jit(solution)/shard_map/ppermute | solution.py:289
  42.8 15.3 %collective-permute-start.7 = (f32[520,128]{1,0:T(8,128)S(1)}, f32[520,128]{1,0:T(8,128)S(1)}, u32[]{:S(2)}, u32[]{:S(2)}) collective-permute-start(f32[520,128]{1,0:T(8,128)S(1)} %shard_map.73.odd.state.before), channel_id=1, source_target_pairs={{0,510},{1,3},{2,0},{3,5},{4,2},{5,7},{6,4},{7,9},{8,6},{9,11},{10... | collective-permute-start | bytes 798728 | tf_op jit(solution)/shard_map/ppermute | solution.py:289
  45.6 20.3 %collective-permute-start.8 = (f32[520,128]{1,0:T(8,128)S(1)}, f32[520,128]{1,0:T(8,128)S(1)}, u32[]{:S(2)}, u32[]{:S(2)}) collective-permute-start(f32[520,128]{1,0:T(8,128)S(1)} %shard_map.72.even.state.before), channel_id=1, source_target_pairs={{0,2},{1,511},{2,4},{3,1},{4,6},{5,3},{6,8},{7,5},{8,10},{9,7},{10... | collective-permute-start | bytes 798728 | tf_op jit(solution)/shard_map/ppermute | solution.py:289
  59.0 14.1 %collective-permute-start.10 = (f32[520,128]{1,0:T(8,128)S(1)}, f32[520,128]{1,0:T(8,128)S(1)}, u32[]{:S(2)}, u32[]{:S(2)}) collective-permute-start(f32[520,128]{1,0:T(8,128)S(1)} %shard_map.75.even.state), channel_id=1, source_target_pairs={{0,2},{1,511},{2,4},{3,1},{4,6},{5,3},{6,8},{7,5},{8,10},{9,7},{10... | collective-permute-start | bytes 798728 | tf_op jit(solution)/shard_map/ppermute | solution.py:289
  66.8 15.9 %collective-permute-start.9 = (f32[520,128]{1,0:T(8,128)S(1)}, f32[520,128]{1,0:T(8,128)S(1)}, u32[]{:S(2)}, u32[]{:S(2)}) collective-permute-start(f32[520,128]{1,0:T(8,128)S(1)} %shard_map.76.odd.state), channel_id=1, source_target_pairs={{0,510},{1,3},{2,0},{3,5},{4,2},{5,7},{6,4},{7,9},{8,6},{9,11},{10... | collective-permute-start | bytes 798728 | tf_op jit(solution)/shard_map/ppermute | solution.py:289
  83.7 28.6 %collective-permute-start.12 = (f32[8,32,128]{2,1,0:T(8,128)S(1)}, f32[8,32,128]{2,1,0:T(8,128)S(1)}, u32[]{:S(2)}, u32[]{:S(2)}) collective-permute-start(f32[8,32,128]{2,1,0:T(8,128)S(1)} %get-tuple-element.49), channel_id=1, source_target_pairs={{0,2},{1,7},{2,4},{3,1},{4,6},{5,3},{6,0},{7,5},{8,10},{9,15},{10,... | collective-permute-start | bytes 393224 | tf_op jit(solution)/shard_map/ppermute | solution.py:283
  89.3 23.0 %collective-permute-start.13 = (f32[8,32,128]{2,1,0:T(8,128)S(1)}, f32[8,32,128]{2,1,0:T(8,128)S(1)}, u32[]{:S(2)}, u32[]{:S(2)}) collective-permute-start(f32[8,32,128]{2,1,0:T(8,128)S(1)} %get-tuple-element.50), channel_id=1, source_target_pairs={{0,4},{1,5},{2,6},{3,7},{4,0},{5,1},{6,2},{7,3},{8,12},{9,13},{10,... | collective-permute-start | bytes 393224 | tf_op jit(solution)/shard_map/ppermute | solution.py:283
  107.3 7.8 %collective-permute-start.14 = (f32[8,32,128]{2,1,0:T(8,128)S(1)}, f32[8,32,128]{2,1,0:T(8,128)S(1)}, u32[]{:S(2)}, u32[]{:S(2)}) collective-permute-start(f32[8,32,128]{2,1,0:T(8,128)S(1)} %get-tuple-element.51), channel_id=1, source_target_pairs={{0,6},{1,3},{2,0},{3,5},{4,2},{5,7},{6,4},{7,1},{8,14},{9,11},{10,... | collective-permute-start | bytes 393224 | tf_op jit(solution)/shard_map/ppermute | solution.py:283
  109.2 3.1 %collective-permute-start.11 = (f32[8,128]{1,0:T(8,128)S(1)}, f32[8,128]{1,0:T(8,128)S(1)}, u32[]{:S(2)}, u32[]{:S(2)}) collective-permute-start(f32[8,128]{1,0:T(8,128)S(1)} %get-tuple-element.47.checks), channel_id=1, source_target_pairs={{0,1},{1,0},{2,3},{3,2},{4,5},{5,4},{6,7},{7,6},{8,9},{9,8},{10,11... | collective-permute-start | bytes 12296 | tf_op jit(solution)/shard_map/ppermute | solution.py:256

commit v4 on v3

--- a/solution.py
+++ b/solution.py
@@ -193,20 +193,35 @@
 
 def gather_kernel(order, weights, *refs):
     del order
-    parts = weights.shape[0] // refs[0].shape[1]
-    pieces, halves = refs[:parts], refs[parts:]
+    parts, (column, line, semaphore) = lax.axis_size("part"), refs[-3:]
+    pieces, halves = refs[:parts], refs[parts:-3]
+    copy = pltpu.make_async_copy(weights, line, semaphore)
+    copy.start()
     each = pieces[0].shape[1]
     width = parts * each
-    for half, start in zip(halves, (swap_here(), REACH - swap_here())):
+    starts = (swap_here(), REACH - swap_here())
+    for half, start in zip(halves, starts):
+        for steps, piece in enumerate(pieces):
+            at = pl.multiple_of(part_from(-steps) * each, each)
+            for tile in range(REACH):
+                half[pl.ds(tile * width + at, each), :] = piece[start + tile]
+    copy.wait()
+    shape = (B, line.shape[1])
+    for first in range(0, line.shape[1], B):
+        at = first + lax.broadcasted_iota(jnp.int32, shape, 0)
+        chosen = at == lax.broadcasted_iota(jnp.int32, shape, 1)
+        value = jnp.sum(jnp.where(chosen, line[...], 0.0), axis=1, keepdims=True)
+        column[first : first + B, :] = jnp.broadcast_to(value, (B, B))
+    for half, start in zip(halves, starts):
+        rows = [jnp.zeros((1, B), jnp.float32)] * REACH
+        for steps, piece in enumerate(pieces):
+            group = (part_from(-steps) * CORES + lax.axis_index("core")) * each
+            factors = column[pl.ds(pl.multiple_of(group, each), each), :]
+            for tile in range(REACH):
+                terms = piece[start + tile] * factors
+                rows[tile] = rows[tile] + jnp.sum(terms, axis=0, keepdims=True)
         for tile in range(REACH):
-            row = jnp.zeros((1, B), jnp.float32)
-            for steps, piece in enumerate(pieces):
-                at = pl.multiple_of(part_from(-steps) * each, each)
-                value = piece[start + tile]
-                row = row + jnp.sum(value * weights[pl.ds(at, each), :], axis=0, keepdims=True)
-                half[pl.ds(tile * width + at, each), :] = value
-            spot = REACH * width + tile
-            half[spot : spot + 1, :] = row
+            half[REACH * width + tile : REACH * width + tile + 1, :] = rows[tile]
 
 
 def arrange_kernel(vectors, *refs):
@@ -305,13 +320,17 @@
         [(place, SMEM), (ints, SMEM), (other_ints, SMEM), (pltpu.with_memory_space_constraint(ham_blocks, pltpu.HBM), HBM), (other_blocks, VMEM)],
         [pltpu.VMEM(ham_blocks.shape, f32), pltpu.SemaphoreType.DMA((rows,))],
     )
-    mine = lax.dynamic_index_in_dim(check_weights.reshape(parts, CORES, each), core, 1, False)
-    weights = jnp.broadcast_to(mine.reshape(width, 1), (width, B))
     full = ((REACH * width + CHECK, B), f32, VMEM)
     even, odd = call(
         gather_kernel,
         (full, full),
-        [(near_list, ANY), (weights, VMEM)] + [(value, VMEM) for value in arrived],
+        [(other_ints, ANY), (pltpu.with_memory_space_constraint(check_weights[None, :], pltpu.HBM), HBM)]
+        + [(value, VMEM) for value in arrived],
+        [
+            pltpu.VMEM((check_weights.shape[0], B), f32),
+            pltpu.VMEM((1, check_weights.shape[0]), f32),
+            pltpu.SemaphoreType.DMA(()),
+        ],
     )
     even_before, odd_before = even, odd
     list_scratch = [pltpu.SMEM(list_shape[0], jnp.int32), pltpu.SemaphoreType.DMA(())]

time: 117 us -> 110 us (0.940)
  the two profiles are of different devices: /device:TPU:206 before, /device:TPU:263 now
where the time goes in v4:
time: 110 us; the launch traced here: 108 us
  starting transfers between devices  75.3 us (68%)
  Pallas kernels  16.9 us (15%)
  waiting for transfers between devices  13.7 us (12%)
    ppermute x6, starting transfers between devices, exchange(): lax.ppermute(pieces[steps], ('part', 'core'), pairs(parts, steps))  37.9 us
    ppermute x3, starting transfers between devices, shift(): lax.ppermute(value, axes, [(at, (at + steps) % count) for at in range(cou...  18.9 us
    ppermute x6, starting transfers between devices, round_chips(): return lax.ppermute(value, ('row', 'part', 'core'), pairs(chips, steps))  18.5 us
    pallas_call x13, Pallas kernels, call(): pl.pallas_call(kernel, out_shape=tuple((jax.ShapeDtypeStruct(shape, dtype...  16.9 us
    ppermute x6, waiting for transfers between devices, round_chips(): return lax.ppermute(value, ('row', 'part', 'core'), pairs(chips, steps))  12.1 us
  transfers between devices with their start and end apart: 15, of which 5 were waited for; matrix products, arithmetic and copies ran while one was open for 1% of the time, Pallas kernels for 13%

profile of v4, /device:TPU:263, one launch (start us, length us, event | category | flops | bytes accessed | tf_op | source)
XLA Modules:
  0.0 108.3 jit_solution(12300451407751240334)
XLA Ops:
  0.6 1.3 %shard_map.68 = (f32[8,32,128]{2,1,0:T(8,128)S(1)}, f32[8,32,128]{2,1,0:T(8,128)S(1)}, f32[8,32,128]{2,1,0:T(8,128)S(1)}, f32[8,32,128]{2,1,0:T(8,128)S(1)}) custom-call(f32[32,4096]{1,0:T(8,128)} %bitcast.10), custom_call_target="tpu_custom_call" | custom-call | flops 1 | bytes 1 | tf_op jit(solution)/shard_map/pallas_call | solution.py:259
  1.9 2.6 %collective-permute-start.4 = (f32[4,8,128,128]{3,2,1,0:T(8,128)}, f32[4,8,128,128]{3,2,1,0:T(8,128)S(1)}, u32[]{:S(2)}, u32[]{:S(2)}) collective-permute-start(f32[4,8,128,128]{3,2,1,0:T(8,128)} %source.1), channel_id=1, source_target_pairs={{0,1},{1,0},{2,3},{3,2},{4,5},{5,4},{6,7},{7,6},{8,9},{9,8},{10,11... | collective-permute-start | bytes 6291464 | tf_op jit(solution)/shard_map/ppermute | solution.py:271
  4.5 5.9 %collective-permute-start.1 = (f32[8,32,128]{2,1,0:T(8,128)S(1)}, f32[8,32,128]{2,1,0:T(8,128)S(1)}, u32[]{:S(2)}, u32[]{:S(2)}) collective-permute-start(f32[8,32,128]{2,1,0:T(8,128)S(1)} %get-tuple-element.31), channel_id=1, source_target_pairs={{0,2},{1,7},{2,4},{3,1},{4,6},{5,3},{6,0},{7,5},{8,10},{9,15},{10,... | collective-permute-start | bytes 393224 | tf_op jit(solution)/shard_map/ppermute | solution.py:298
  10.4 3.5 %collective-permute-start.2 = (f32[8,32,128]{2,1,0:T(8,128)S(1)}, f32[8,32,128]{2,1,0:T(8,128)S(1)}, u32[]{:S(2)}, u32[]{:S(2)}) collective-permute-start(f32[8,32,128]{2,1,0:T(8,128)S(1)} %get-tuple-element.32), channel_id=1, source_target_pairs={{0,4},{1,5},{2,6},{3,7},{4,0},{5,1},{6,2},{7,3},{8,12},{9,13},{10,... | collective-permute-start | bytes 393224 | tf_op jit(solution)/shard_map/ppermute | solution.py:298
  14.0 4.2 %collective-permute-start.3 = (f32[8,32,128]{2,1,0:T(8,128)S(1)}, f32[8,32,128]{2,1,0:T(8,128)S(1)}, u32[]{:S(2)}, u32[]{:S(2)}) collective-permute-start(f32[8,32,128]{2,1,0:T(8,128)S(1)} %get-tuple-element.33), channel_id=1, source_target_pairs={{0,6},{1,3},{2,0},{3,5},{4,2},{5,7},{6,4},{7,1},{8,14},{9,11},{10,... | collective-permute-start | bytes 393224 | tf_op jit(solution)/shard_map/ppermute | solution.py:298
  18.2 0.7 pad_bitcast_fusion
  18.9 0.7 pad_add_fusion.ints_own
  19.5 4.0 %collective-permute-start = (s32[5,8]{1,0:T(8,128)S(1)}, s32[5,8]{1,0:T(8,128)S(1)}, u32[]{:S(2)}, u32[]{:S(2)}) collective-permute-start(s32[5,8]{1,0:T(8,128)S(1)} %pad_add_fusion.ints_own), channel_id=1, source_target_pairs={{0,1},{1,0},{2,3},{3,2},{4,5},{5,4},{6,7},{7,6},{8,9},{9,8},{10,11... | collective-permute-start | bytes 488 | tf_op jit(solution)/shard_map/ppermute | solution.py:271
  23.5 0.8 collective-permute-done.order.ints_other
  24.3 0.0 collective-permute-done.1.refs_1_
  24.3 0.0 collective-permute-done.2.refs_2_
  24.3 0.0 collective-permute-done.3.refs_3_
  24.3 0.9 shard_map.69
  25.2 3.2 %collective-permute-start.6 = (f32[520,128]{1,0:T(8,128)S(1)}, f32[520,128]{1,0:T(8,128)S(1)}, u32[]{:S(2)}, u32[]{:S(2)}) collective-permute-start(f32[520,128]{1,0:T(8,128)S(1)} %get-tuple-element.34.even.state.before), channel_id=1, source_target_pairs={{0,2},{1,511},{2,4},{3,1},{4,6},{5,3},{6,8},{7,5},{8,10},{9,7},{10... | collective-permute-start | bytes 798728 | tf_op jit(solution)/shard_map/ppermute | solution.py:304
  28.4 3.0 %collective-permute-start.5 = (f32[520,128]{1,0:T(8,128)S(1)}, f32[520,128]{1,0:T(8,128)S(1)}, u32[]{:S(2)}, u32[]{:S(2)}) collective-permute-start(f32[520,128]{1,0:T(8,128)S(1)} %get-tuple-element.35.odd.state.before), channel_id=1, source_target_pairs={{0,510},{1,3},{2,0},{3,5},{4,2},{5,7},{6,4},{7,9},{8,6},{9,11},{10... | collective-permute-start | bytes 798728 | tf_op jit(solution)/shard_map/ppermute | solution.py:304
  31.4 0.1 pad_add_fusion.1.place
  31.5 0.0 collective-permute-done.4.other
  31.5 3.5 %shard_map.70 = (bf16[65,128,256]{2,1,0:T(8,128)(2,1)S(1)}, s32[4,68]{1,0:T(4,128)S(1)}, s32[4,68]{1,0:T(4,128)S(1)}, s32[4,68]{1,0:T(4,128)S(1)}) custom-call(s32[4]{0:T(128)S(1)} %pad_add_fusion.1.place, s32[5,8]{1,0:T(8,128)S(1)} %pad_add_fusion.ints_own, s32[5,8]{1,0:T(8,128)S(1)} %collective-permute-done.order.ints_other, f32[4,8,128,128]{3,2,1,0:T(8,128)} %source.1, ...), custom_call_target="tpu_custom_call" | custom-call | flops 1 | bytes 1 | tf_op jit(solution)/shard_map/pallas_call | solution.py:259
  35.0 1.6 %shard_map.71 = (f32[4,144,128]{2,1,0:T(8,128)S(1)}, f32[4,144,128]{2,1,0:T(8,128)S(1)}) custom-call(f32[520,128]{1,0:T(8,128)S(1)} %get-tuple-element.34.even.state.before, f32[520,128]{1,0:T(8,128)S(1)} %get-tuple-element.35.odd.state.before, s32[4,68]{1,0:T(4,128)S(1)} %get-tuple-element.37.listed, bf16[65,128,256]{2,1,0:T(8,128)(2,1)S(1)} %get-tuple-element.38.rhs), custom_call_target="tpu_custom_call" | custom-call | flops 1 | bytes 1 | tf_op jit(solution)/shard_map/pallas_call | solution.py:259
  36.6 0.0 collective-permute-done.6.halo
  36.6 0.9 shard_map.73.odd.state.before
  37.5 3.0 %collective-permute-start.7 = (f32[520,128]{1,0:T(8,128)S(1)}, f32[520,128]{1,0:T(8,128)S(1)}, u32[]{:S(2)}, u32[]{:S(2)}) collective-permute-start(f32[520,128]{1,0:T(8,128)S(1)} %shard_map.73.odd.state.before), channel_id=1, source_target_pairs={{0,510},{1,3},{2,0},{3,5},{4,2},{5,7},{6,4},{7,9},{8,6},{9,11},{10... | collective-permute-start | bytes 798728 | tf_op jit(solution)/shard_map/ppermute | solution.py:304
  40.5 4.1 %collective-permute-done.5.halo = f32[520,128]{1,0:T(8,128)S(1)} collective-permute-done((f32[520,128]{1,0:T(8,128)S(1)}, f32[520,128]{1,0:T(8,128)S(1)}, u32[]{:S(2)}, u32[]{:S(2)}) %collective-permute-start.5) | collective-permute-done | bytes 266272 | tf_op jit(solution)/shard_map/ppermute | solution.py:304
  44.7 0.9 shard_map.72.even.state.before
  45.6 3.8 %collective-permute-start.8 = (f32[520,128]{1,0:T(8,128)S(1)}, f32[520,128]{1,0:T(8,128)S(1)}, u32[]{:S(2)}, u32[]{:S(2)}) collective-permute-start(f32[520,128]{1,0:T(8,128)S(1)} %shard_map.72.even.state.before), channel_id=1, source_target_pairs={{0,2},{1,511},{2,4},{3,1},{4,6},{5,3},{6,8},{7,5},{8,10},{9,7},{10... | collective-permute-start | bytes 798728 | tf_op jit(solution)/shard_map/ppermute | solution.py:304
  49.4 1.6 %shard_map.74 = (f32[4,144,128]{2,1,0:T(8,128)S(1)}, f32[4,144,128]{2,1,0:T(8,128)S(1)}) custom-call(f32[520,128]{1,0:T(8,128)S(1)} %shard_map.72.even.state.before, f32[520,128]{1,0:T(8,128)S(1)} %shard_map.73.odd.state.before, s32[4,68]{1,0:T(4,128)S(1)} %get-tuple-element.37.listed, bf16[65,128,256]{2,1,0:T(8,128)(2,1)S(1)} %get-tuple-element.38.rhs), custom_call_target="tpu_custom_call" | custom-call | flops 1 | bytes 1 | tf_op jit(solution)/shard_map/pallas_call | solution.py:259
  51.1 0.0 collective-permute-done.7.halo
  51.1 0.9 shard_map.75.even.state
  52.0 2.2 %collective-permute-start.10 = (f32[520,128]{1,0:T(8,128)S(1)}, f32[520,128]{1,0:T(8,128)S(1)}, u32[]{:S(2)}, u32[]{:S(2)}) collective-permute-start(f32[520,128]{1,0:T(8,128)S(1)} %shard_map.75.even.state), channel_id=1, source_target_pairs={{0,2},{1,511},{2,4},{3,1},{4,6},{5,3},{6,8},{7,5},{8,10},{9,7},{10... | collective-permute-start | bytes 798728 | tf_op jit(solution)/shard_map/ppermute | solution.py:304
  54.2 2.6 %collective-permute-done.8.halo = f32[520,128]{1,0:T(8,128)S(1)} collective-permute-done((f32[520,128]{1,0:T(8,128)S(1)}, f32[520,128]{1,0:T(8,128)S(1)}, u32[]{:S(2)}, u32[]{:S(2)}) %collective-permute-start.8) | collective-permute-done | bytes 266272 | tf_op jit(solution)/shard_map/ppermute | solution.py:304
  56.8 0.9 shard_map.76.odd.state
  57.7 3.3 %collective-permute-start.9 = (f32[520,128]{1,0:T(8,128)S(1)}, f32[520,128]{1,0:T(8,128)S(1)}, u32[]{:S(2)}, u32[]{:S(2)}) collective-permute-start(f32[520,128]{1,0:T(8,128)S(1)} %shard_map.76.odd.state), channel_id=1, source_target_pairs={{0,510},{1,3},{2,0},{3,5},{4,2},{5,7},{6,4},{7,9},{8,6},{9,11},{10... | collective-permute-start | bytes 798728 | tf_op jit(solution)/shard_map/ppermute | solution.py:304
  61.0 1.6 %shard_map.77 = (f32[4,144,128]{2,1,0:T(8,128)S(1)}, f32[4,144,128]{2,1,0:T(8,128)S(1)}) custom-call(f32[520,128]{1,0:T(8,128)S(1)} %shard_map.75.even.state, f32[520,128]{1,0:T(8,128)S(1)} %shard_map.76.odd.state, s32[4,68]{1,0:T(4,128)S(1)} %get-tuple-element.37.listed, bf16[65,128,256]{2,1,0:T(8,128)(2,1)S(1)} %get-tuple-element.38.rhs), custom_call_target="tpu_custom_call" | custom-call | flops 1 | bytes 1 | tf_op jit(solution)/shard_map/pallas_call | solution.py:259
  62.6 0.0 collective-permute-done.10.halo
  62.6 0.9 shard_map.78.odd
  63.6 5.4 %collective-permute-done.9.halo = f32[520,128]{1,0:T(8,128)S(1)} collective-permute-done((f32[520,128]{1,0:T(8,128)S(1)}, f32[520,128]{1,0:T(8,128)S(1)}, u32[]{:S(2)}, u32[]{:S(2)}) %collective-permute-start.9) | collective-permute-done | bytes 266272 | tf_op jit(solution)/shard_map/ppermute | solution.py:304
  68.9 0.9 shard_map.79
  69.9 18.4 %collective-permute-start.12 = (f32[8,32,128]{2,1,0:T(8,128)S(1)}, f32[8,32,128]{2,1,0:T(8,128)S(1)}, u32[]{:S(2)}, u32[]{:S(2)}) collective-permute-start(f32[8,32,128]{2,1,0:T(8,128)S(1)} %get-tuple-element.49), channel_id=1, source_target_pairs={{0,2},{1,7},{2,4},{3,1},{4,6},{5,3},{6,0},{7,5},{8,10},{9,15},{10,... | collective-permute-start | bytes 393224 | tf_op jit(solution)/shard_map/ppermute | solution.py:298
  88.3 1.9 %collective-permute-start.13 = (f32[8,32,128]{2,1,0:T(8,128)S(1)}, f32[8,32,128]{2,1,0:T(8,128)S(1)}, u32[]{:S(2)}, u32[]{:S(2)}) collective-permute-start(f32[8,32,128]{2,1,0:T(8,128)S(1)} %get-tuple-element.50), channel_id=1, source_target_pairs={{0,4},{1,5},{2,6},{3,7},{4,0},{5,1},{6,2},{7,3},{8,12},{9,13},{10,... | collective-permute-start | bytes 393224 | tf_op jit(solution)/shard_map/ppermute | solution.py:298
  90.2 4.0 %collective-permute-start.14 = (f32[8,32,128]{2,1,0:T(8,128)S(1)}, f32[8,32,128]{2,1,0:T(8,128)S(1)}, u32[]{:S(2)}, u32[]{:S(2)}) collective-permute-start(f32[8,32,128]{2,1,0:T(8,128)S(1)} %get-tuple-element.51), channel_id=1, source_target_pairs={{0,6},{1,3},{2,0},{3,5},{4,2},{5,7},{6,4},{7,1},{8,14},{9,11},{10,... | collective-permute-start | bytes 393224 | tf_op jit(solution)/shard_map/ppermute | solution.py:298
  94.2 12.3 %collective-permute-start.11 = (f32[8,128]{1,0:T(8,128)S(1)}, f32[8,128]{1,0:T(8,128)S(1)}, u32[]{:S(2)}, u32[]{:S(2)}) collective-permute-start(f32[8,128]{1,0:T(8,128)S(1)} %get-tuple-element.47.checks), channel_id=1, source_target_pairs={{0,1},{1,0},{2,3},{3,2},{4,5},{5,4},{6,7},{7,6},{8,9},{9,8},{10,11... | collective-permute-start | bytes 12296 | tf_op jit(solution)/shard_map/ppermute | solution.py:271
  106.6 0.8 collective-permute-done.11.other_checks
  107.4 0.0 collective-permute-done.12.refs_1_
  107.4 0.0 collective-permute-done.13.refs_2_
  107.4 0.0 collective-permute-done.14.refs_3_
  107.4 0.9 shard_map.80
Async XLA Ops:
  1.9 29.5 %collective-permute-start.4 = (f32[4,8,128,128]{3,2,1,0:T(8,128)}, f32[4,8,128,128]{3,2,1,0:T(8,128)S(1)}, u32[]{:S(2)}, u32[]{:S(2)}) collective-permute-start(f32[4,8,128,128]{3,2,1,0:T(8,128)} %source.1), channel_id=1, source_target_pairs={{0,1},{1,0},{2,3},{3,2},{4,5},{5,4},{6,7},{7,6},{8,9},{9,8},{10,11... | collective-permute-start | bytes 6291464 | tf_op jit(solution)/shard_map/ppermute | solution.py:271
  4.5 19.8 %collective-permute-start.1 = (f32[8,32,128]{2,1,0:T(8,128)S(1)}, f32[8,32,128]{2,1,0:T(8,128)S(1)}, u32[]{:S(2)}, u32[]{:S(2)}) collective-permute-start(f32[8,32,128]{2,1,0:T(8,128)S(1)} %get-tuple-element.31), channel_id=1, source_target_pairs={{0,2},{1,7},{2,4},{3,1},{4,6},{5,3},{6,0},{7,5},{8,10},{9,15},{10,... | collective-permute-start | bytes 393224 | tf_op jit(solution)/shard_map/ppermute | solution.py:298
  10.4 13.9 %collective-permute-start.2 = (f32[8,32,128]{2,1,0:T(8,128)S(1)}, f32[8,32,128]{2,1,0:T(8,128)S(1)}, u32[]{:S(2)}, u32[]{:S(2)}) collective-permute-start(f32[8,32,128]{2,1,0:T(8,128)S(1)} %get-tuple-element.32), channel_id=1, source_target_pairs={{0,4},{1,5},{2,6},{3,7},{4,0},{5,1},{6,2},{7,3},{8,12},{9,13},{10,... | collective-permute-start | bytes 393224 | tf_op jit(solution)/shard_map/ppermute | solution.py:298
  14.0 10.4 %collective-permute-start.3 = (f32[8,32,128]{2,1,0:T(8,128)S(1)}, f32[8,32,128]{2,1,0:T(8,128)S(1)}, u32[]{:S(2)}, u32[]{:S(2)}) collective-permute-start(f32[8,32,128]{2,1,0:T(8,128)S(1)} %get-tuple-element.33), channel_id=1, source_target_pairs={{0,6},{1,3},{2,0},{3,5},{4,2},{5,7},{6,4},{7,1},{8,14},{9,11},{10,... | collective-permute-start | bytes 393224 | tf_op jit(solution)/shard_map/ppermute | solution.py:298
  19.5 4.8 %collective-permute-start = (s32[5,8]{1,0:T(8,128)S(1)}, s32[5,8]{1,0:T(8,128)S(1)}, u32[]{:S(2)}, u32[]{:S(2)}) collective-permute-start(s32[5,8]{1,0:T(8,128)S(1)} %pad_add_fusion.ints_own), channel_id=1, source_target_pairs={{0,1},{1,0},{2,3},{3,2},{4,5},{5,4},{6,7},{7,6},{8,9},{9,8},{10,11... | collective-permute-start | bytes 488 | tf_op jit(solution)/shard_map/ppermute | solution.py:271
  25.2 11.4 %collective-permute-start.6 = (f32[520,128]{1,0:T(8,128)S(1)}, f32[520,128]{1,0:T(8,128)S(1)}, u32[]{:S(2)}, u32[]{:S(2)}) collective-permute-start(f32[520,128]{1,0:T(8,128)S(1)} %get-tuple-element.34.even.state.before), channel_id=1, source_target_pairs={{0,2},{1,511},{2,4},{3,1},{4,6},{5,3},{6,8},{7,5},{8,10},{9,7},{10... | collective-permute-start | bytes 798728 | tf_op jit(solution)/shard_map/ppermute | solution.py:304
  28.4 16.2 %collective-permute-start.5 = (f32[520,128]{1,0:T(8,128)S(1)}, f32[520,128]{1,0:T(8,128)S(1)}, u32[]{:S(2)}, u32[]{:S(2)}) collective-permute-start(f32[520,128]{1,0:T(8,128)S(1)} %get-tuple-element.35.odd.state.before), channel_id=1, source_target_pairs={{0,510},{1,3},{2,0},{3,5},{4,2},{5,7},{6,4},{7,9},{8,6},{9,11},{10... | collective-permute-start | bytes 798728 | tf_op jit(solution)/shard_map/ppermute | solution.py:304
  37.5 13.5 %collective-permute-start.7 = (f32[520,128]{1,0:T(8,128)S(1)}, f32[520,128]{1,0:T(8,128)S(1)}, u32[]{:S(2)}, u32[]{:S(2)}) collective-permute-start(f32[520,128]{1,0:T(8,128)S(1)} %shard_map.73.odd.state.before), channel_id=1, source_target_pairs={{0,510},{1,3},{2,0},{3,5},{4,2},{5,7},{6,4},{7,9},{8,6},{9,11},{10... | collective-permute-start | bytes 798728 | tf_op jit(solution)/shard_map/ppermute | solution.py:304
  45.6 11.2 %collective-permute-start.8 = (f32[520,128]{1,0:T(8,128)S(1)}, f32[520,128]{1,0:T(8,128)S(1)}, u32[]{:S(2)}, u32[]{:S(2)}) collective-permute-start(f32[520,128]{1,0:T(8,128)S(1)} %shard_map.72.even.state.before), channel_id=1, source_target_pairs={{0,2},{1,511},{2,4},{3,1},{4,6},{5,3},{6,8},{7,5},{8,10},{9,7},{10... | collective-permute-start | bytes 798728 | tf_op jit(solution)/shard_map/ppermute | solution.py:304
  52.0 10.6 %collective-permute-start.10 = (f32[520,128]{1,0:T(8,128)S(1)}, f32[520,128]{1,0:T(8,128)S(1)}, u32[]{:S(2)}, u32[]{:S(2)}) collective-permute-start(f32[520,128]{1,0:T(8,128)S(1)} %shard_map.75.even.state), channel_id=1, source_target_pairs={{0,2},{1,511},{2,4},{3,1},{4,6},{5,3},{6,8},{7,5},{8,10},{9,7},{10... | collective-permute-start | bytes 798728 | tf_op jit(solution)/shard_map/ppermute | solution.py:304
  57.7 11.2 %collective-permute-start.9 = (f32[520,128]{1,0:T(8,128)S(1)}, f32[520,128]{1,0:T(8,128)S(1)}, u32[]{:S(2)}, u32[]{:S(2)}) collective-permute-start(f32[520,128]{1,0:T(8,128)S(1)} %shard_map.76.odd.state), channel_id=1, source_target_pairs={{0,510},{1,3},{2,0},{3,5},{4,2},{5,7},{6,4},{7,9},{8,6},{9,11},{10... | collective-permute-start | bytes 798728 | tf_op jit(solution)/shard_map/ppermute | solution.py:304
  69.9 37.5 %collective-permute-start.12 = (f32[8,32,128]{2,1,0:T(8,128)S(1)}, f32[8,32,128]{2,1,0:T(8,128)S(1)}, u32[]{:S(2)}, u32[]{:S(2)}) collective-permute-start(f32[8,32,128]{2,1,0:T(8,128)S(1)} %get-tuple-element.49), channel_id=1, source_target_pairs={{0,2},{1,7},{2,4},{3,1},{4,6},{5,3},{6,0},{7,5},{8,10},{9,15},{10,... | collective-permute-start | bytes 393224 | tf_op jit(solution)/shard_map/ppermute | solution.py:298
  88.3 19.1 %collective-permute-start.13 = (f32[8,32,128]{2,1,0:T(8,128)S(1)}, f32[8,32,128]{2,1,0:T(8,128)S(1)}, u32[]{:S(2)}, u32[]{:S(2)}) collective-permute-start(f32[8,32,128]{2,1,0:T(8,128)S(1)} %get-tuple-element.50), channel_id=1, source_target_pairs={{0,4},{1,5},{2,6},{3,7},{4,0},{5,1},{6,2},{7,3},{8,12},{9,13},{10,... | collective-permute-start | bytes 393224 | tf_op jit(solution)/shard_map/ppermute | solution.py:298
  90.2 17.2 %collective-permute-start.14 = (f32[8,32,128]{2,1,0:T(8,128)S(1)}, f32[8,32,128]{2,1,0:T(8,128)S(1)}, u32[]{:S(2)}, u32[]{:S(2)}) collective-permute-start(f32[8,32,128]{2,1,0:T(8,128)S(1)} %get-tuple-element.51), channel_id=1, source_target_pairs={{0,6},{1,3},{2,0},{3,5},{4,2},{5,7},{6,4},{7,1},{8,14},{9,11},{10,... | collective-permute-start | bytes 393224 | tf_op jit(solution)/shard_map/ppermute | solution.py:298
  94.2 13.2 %collective-permute-start.11 = (f32[8,128]{1,0:T(8,128)S(1)}, f32[8,128]{1,0:T(8,128)S(1)}, u32[]{:S(2)}, u32[]{:S(2)}) collective-permute-start(f32[8,128]{1,0:T(8,128)S(1)} %get-tuple-element.47.checks), channel_id=1, source_target_pairs={{0,1},{1,0},{2,3},{3,2},{4,5},{5,4},{6,7},{7,6},{8,9},{9,8},{10,11... | collective-permute-start | bytes 12296 | tf_op jit(solution)/shard_map/ppermute | solution.py:271
